TPU v7x, 512 devices: a whole 4x8x8 slice. The times are simulated.
512 devices in a mesh: row: 16 (over y, core), col: 32 (over z, x).
Axes of the slice: x: 4, y: 8, z: 8, core: 2. Of those that a mesh axis runs over, the one named last changes fastest.
Arguments:
- stream_speed: bfloat16 [512, 2048, 128], P('col', 'row'), may hold values from -6 to 6
- normal_speed: bfloat16 [512, 2048, 128], P('col', 'row'), may hold values from -6 to 6
- span_speed: bfloat16 [512, 2048, 128], P('col', 'row'), may hold values from -6 to 6
- stream_first: bfloat16 [2048, 2048], P('row'), may hold values from -0.125 to 0.125
- stream_second: bfloat16 [2048, 2048], P('row'), may hold values from -0.125 to 0.125
- wall_first: bfloat16 [512, 512], replicated, may hold values from -0.25 to 0.25
- wall_second: bfloat16 [512, 512], replicated, may hold values from -0.25 to 0.25
- metric1: float32 [512], replicated, may hold values from 0.5 to 2
- metric2: float32 [512], replicated, may hold values from -1.5 to 1.5
- span_coef: float32 [2, 9], replicated, may hold values from -1 to 1
- counts: int32 [32], replicated, may hold values from 1 to 4, as said below
Outputs:
- tendency: bfloat16 [512, 2048, 128], P('col', 'row')
Inputs may be any that keep to these rules, and one draw needn't show every extreme that they name: counts[b] is the number of fluid planes at the start of spanwise block b of 4 planes; some block is all fluid.
All inputs are finite; a program needn't handle non-finite values.
Results may differ from a plain program's by a relative error of at most 0.0051.
Values may be sent and summed in bfloat16 or wider, within the bound.
A program may use at most 128 MiB of HBM per device.

v0:
```python
import jax
import jax.numpy as jnp
from jax import lax
from jax.sharding import PartitionSpec as P

ZB = 4


viscosity = 0.25


def wall_terms(speeds, wall_first, wall_second, metric1, metric2):
    stream_lines, normal_lines = speeds
    line_count = stream_lines.shape[0]
    flattened = stream_lines.reshape(line_count, -1)
    product = (
        (stream_lines.astype(jnp.float32) * normal_lines.astype(jnp.float32))
        .astype(jnp.bfloat16)
        .reshape(line_count, -1)
    )
    first_stream = jnp.dot(wall_first, flattened, preferred_element_type=jnp.float32)
    second_stream = jnp.dot(wall_second, flattened, preferred_element_type=jnp.float32)
    first_flux = jnp.dot(wall_first, product, preferred_element_type=jnp.float32)
    weight_one = metric1[:, None]
    weight_two = metric2[:, None]
    outcome = (
        viscosity * (weight_one * weight_one * second_stream + weight_two * first_stream)
        - weight_one * first_flux
    )
    return outcome.astype(jnp.bfloat16).reshape(stream_lines.shape)


def on_device(
    stream_speed,
    normal_speed,
    span_speed,
    stream_first,
    stream_second,
    wall_first,
    wall_second,
    metric1,
    metric2,
    span_coef,
    counts,
):
    normal_local, stream_local, span_total = stream_speed.shape
    gathered = lax.all_gather(stream_speed, "row", axis=1, tiled=True)
    gathered_full = gathered.astype(jnp.float32)
    flux_gathered = (gathered_full * gathered_full).astype(jnp.bfloat16)
    viscous_stream = jnp.einsum(
        "ax,yxz->yaz", stream_second, gathered, preferred_element_type=jnp.float32
    )
    convective_stream = jnp.einsum(
        "ax,yxz->yaz", stream_first, flux_gathered, preferred_element_type=jnp.float32
    )
    term_stream = viscosity * viscous_stream - convective_stream
    outcome = wall_terms(
        (
            lax.all_to_all(stream_speed, "col", split_axis=1, concat_axis=0, tiled=True),
            lax.all_to_all(normal_speed, "col", split_axis=1, concat_axis=0, tiled=True),
        ),
        wall_first,
        wall_second,
        metric1,
        metric2,
    )
    term_wall = lax.all_to_all(outcome, "col", split_axis=0, concat_axis=1, tiled=True)
    stream_full = stream_speed.astype(jnp.float32)
    flux_span = lax.optimization_barrier(
        (stream_full * span_speed.astype(jnp.float32)).astype(jnp.bfloat16)
    ).astype(jnp.float32)
    radius = span_coef.shape[1] // 2
    term_span = jnp.zeros((normal_local, stream_local, span_total), jnp.float32)
    for offset_z in range(-radius, radius + 1):
        term_span = term_span + viscosity * span_coef[1, offset_z + radius] * jnp.roll(
            stream_full, -offset_z, 2
        )
        term_span = term_span - span_coef[0, offset_z + radius] * jnp.roll(flux_span, -offset_z, 2)
    block_total = counts.shape[0]
    plane_index = jnp.arange(span_total, dtype=jnp.int32)
    owner_block = plane_index // ZB
    owner_table = (
        jnp.arange(block_total, dtype=jnp.int32)[:, None] == owner_block[None, :]
    ).astype(jnp.int32)
    fluid_limit = jnp.sum(owner_table * counts[:, None], axis=0)
    fluid_mask = (plane_index % ZB < fluid_limit).astype(jnp.float32)
    combined = term_stream + term_wall.astype(jnp.float32) + term_span
    return (fluid_mask * combined).astype(jnp.bfloat16)


def solution(mesh):
    placed = (
        P("col", "row", None),
        P("col", "row", None),
        P("col", "row", None),
        P("row", None),
        P("row", None),
        P(),
        P(),
        P(),
        P(),
        P(),
        P(),
    )
    return jax.shard_map(
        on_device, mesh=mesh, in_specs=placed, out_specs=P("col", "row", None), check_vma=False
    )
```

profile of v0, /device:TPU:8, one launch (start us, length us, event | category | flops | bytes accessed | tf_op | source)
XLA Modules:
  0.0 121.4 jit_solution(2605083073068939115)
XLA Ops:
  6.5 0.0 all-gather.2.cloned.1.call-start
  6.5 2.1 %copy.37 = bf16[16,128,128]{1,2,0:T(8,128)(2,1)} copy(bf16[16,128,128]{2,1,0:T(8,128)(2,1)} %param.11) | data formatting | bytes 1048576 | tf_op args[0]
  8.7 0.0 all-gather.2.cloned.1.call-update
  8.7 2.2 %copy.40 = bf16[16,128,128]{2,0,1:T(8,128)(2,1)} copy(bf16[16,128,128]{2,1,0:T(8,128)(2,1)} %param.12) | data formatting | bytes 1048576 | tf_op args[1]
  10.9 13.2 %all-to-all-start.1 = ((bf16[16,128,128]{2,0,1:T(8,128)(2,1)}), bf16[16,128,128]{2,0,1:T(8,128)(2,1)S(1)}, u32[]{:S(2)}, u32[]{:S(2)}) async-start(bf16[16,128,128]{2,0,1:T(8,128)(2,1)} %copy.40), calls=%async_computation.1 | async-start | bytes 1048576 | tf_op jit(solution)/shard_map/all_to_all | solution.py:60
  24.0 2.2 %copy.38 = bf16[16,128,128]{2,0,1:T(8,128)(2,1)} copy(bf16[16,128,128]{2,1,0:T(8,128)(2,1)} %param.11) | data formatting | bytes 1048576 | tf_op args[0]
  26.2 1.3 %copy.47 = bf16[16,128,128]{1,2,0:T(8,128)(2,1)S(1)} copy(bf16[16,128,128]{2,1,0:T(8,128)(2,1)} %param.13) | data formatting | bytes 1048576 | tf_op args[2]
  27.5 1.3 %multiply_convert_fusion.14 = bf16[16,128,128]{1,2,0:T(8,128)(2,1)S(1)} fusion(bf16[16,128,128]{1,2,0:T(8,128)(2,1)S(1)} %copy.47, bf16[16,128,128]{1,2,0:T(8,128)(2,1)} %copy.37), kind=kLoop, calls=%fused_computation.53 | loop fusion | flops 1048576 | bytes 1572864 | tf_op jit(solution)/shard_map/convert_element_type | solution.py:70
  28.8 2.0 %fusion.55 = (f32[1,1]{1,0:T(1,128)}, f32[1,1]{1,0:T(1,128)}, f32[1,1]{1,0:T(1,128)}, f32[1,1]{1,0:T(1,128)}, f32[1,1]{1,0:T(1,128)}, /*index=5*/f32[1,1]{1,0:T(...) fusion(f32[2,9]{1,0:T(2,128)} %param.20), kind=kLoop, calls=%fused_computation.86 | loop fusion | bytes 144 | tf_op jit(solution)/shard_map/slice | solution.py:75
  30.9 0.8 fusion.54
  31.7 0.8 fusion.50
  32.5 0.8 fusion.42
  33.3 0.8 fusion.46
  34.1 1.5 %fusion.47 = (f32[16,128,126]{1,2,0:T(8,128)}, f32[16,128,126]{1,2,0:T(8,128)}) fusion(bf16[16,128,128]{1,2,0:T(8,128)(2,1)S(1)} %multiply_convert_fusion.14), kind=kLoop, calls=%fused_computation.78 | loop fusion | bytes 4128768 | tf_op jit(solution)/shard_map/jit(_roll_static)/slice | solution.py:78
  35.6 1.5 %fusion.51 = (f32[16,128,127]{1,2,0:T(8,128)}, f32[16,128,127]{1,2,0:T(8,128)}) fusion(bf16[16,128,128]{1,2,0:T(8,128)(2,1)S(1)} %multiply_convert_fusion.14), kind=kLoop, calls=%fused_computation.82 | loop fusion | bytes 4161536 | tf_op jit(solution)/shard_map/jit(_roll_static)/slice | solution.py:78
  37.2 4.6 %all-to-all-done.1 = bf16[16,128,128]{2,0,1:T(8,128)(2,1)S(1)} async-done(((bf16[16,128,128]{2,0,1:T(8,128)(2,1)}), bf16[16,128,128]{2,0,1:T(8,128)(2,1)S(1)}, u32[]{:S(2)}, u32[]{:S(2)}) %all-to-all-start.1) | async-done | bytes 524320 | tf_op jit(solution)/shard_map/all_to_all | solution.py:60
  41.8 5.3 %all-to-all-start = ((bf16[16,128,128]{2,0,1:T(8,128)(2,1)}), bf16[16,128,128]{2,0,1:T(8,128)(2,1)}, u32[]{:S(2)}, u32[]{:S(2)}) async-start(bf16[16,128,128]{2,0,1:T(8,128)(2,1)} %copy.38), calls=%async_computation | async-start | bytes 1048576 | tf_op jit(solution)/shard_map/all_to_all | solution.py:59
  52.6 0.1 select_reduce_fusion
  52.7 1.5 %fusion.43 = (f32[16,128,125]{1,2,0:T(8,128)}, f32[16,128,125]{1,2,0:T(8,128)}) fusion(bf16[16,128,128]{1,2,0:T(8,128)(2,1)S(1)} %multiply_convert_fusion.14), kind=kLoop, calls=%fused_computation.74 | loop fusion | bytes 4096000 | tf_op jit(solution)/shard_map/jit(_roll_static)/slice | solution.py:78
  54.2 1.5 %fusion.39 = (f32[16,128,124]{1,2,0:T(8,128)}, f32[16,128,124]{1,2,0:T(8,128)}) fusion(bf16[16,128,128]{1,2,0:T(8,128)(2,1)S(1)} %multiply_convert_fusion.14), kind=kLoop, calls=%fused_computation.70 | loop fusion | bytes 4063232 | tf_op jit(solution)/shard_map/jit(_roll_static)/slice | solution.py:78
  55.7 1.5 %fusion.49 = (f32[16,128,126]{1,2,0:T(8,128)}, f32[16,128,126]{1,2,0:T(8,128)}) fusion(bf16[16,128,128]{1,2,0:T(8,128)(2,1)S(1)} %copy-done.1), kind=kLoop, calls=%fused_computation.80 | loop fusion | bytes 4128768 | tf_op jit(solution)/shard_map/jit(_roll_static)/slice | solution.py:75
  57.2 0.2 copy.41
  57.4 6.8 %all-to-all-done = bf16[16,128,128]{2,0,1:T(8,128)(2,1)} async-done(((bf16[16,128,128]{2,0,1:T(8,128)(2,1)}), bf16[16,128,128]{2,0,1:T(8,128)(2,1)}, u32[]{:S(2)}, u32[]{:S(2)}) %all-to-all-start) | async-done | bytes 524320 | tf_op jit(solution)/shard_map/all_to_all | solution.py:59
  64.3 1.3 %copy.39 = bf16[16,32,4,128]{3,2,0,1:T(4,128)(2,1)S(1)} copy(bf16[16,32,4,128]{3,0,2,1:T(8,128)(2,1)} %bitcast.3) | data formatting | bytes 1048576 | tf_op jit(solution)/shard_map/all_to_all | solution.py:59
  65.6 1.5 %convolution_multiply_fusion.2 = f32[512,512]{0,1:T(8,128)S(1)} fusion(bf16[512,512]{1,0:T(8,128)(2,1)} %param.17, f32[512]{0:T(512)S(1)} %mul.238, bf16[64,8,4,128]{3,2,1,0:T(4,128)(2,1)S(1)} %bitcast.73), kind=kOutput, calls=%fused_computation.8 | convolution fusion | flops 268697600 | bytes 2099200 | tf_op jit(solution)/shard_map/dot_general | solution.py:22
  67.1 0.5 fusion.4
  67.6 0.5 fusion.10
  68.1 1.1 copy.42
  69.2 4.8 %all-to-all-start.2 = ((bf16[512,4,128]{2,1,0:T(4,128)(2,1)}), bf16[512,4,128]{2,1,0:T(4,128)(2,1)S(1)}, u32[]{:S(2)}, u32[]{:S(2)}) async-start(bf16[512,4,128]{2,1,0:T(4,128)(2,1)} %copy.42), calls=%async_computation.2 | async-start | bytes 1048576 | tf_op jit(solution)/shard_map/all_to_all | solution.py:67
  74.0 1.5 %fusion.53 = (f32[16,128,127]{1,2,0:T(8,128)}, f32[16,128,127]{1,2,0:T(8,128)}) fusion(bf16[16,128,128]{1,2,0:T(8,128)(2,1)S(1)} %copy-done.1), kind=kLoop, calls=%fused_computation.84 | loop fusion | bytes 4161536 | tf_op jit(solution)/shard_map/jit(_roll_static)/slice | solution.py:75
  75.5 1.5 %fusion.45 = (f32[16,128,125]{1,2,0:T(8,128)}, f32[16,128,125]{1,2,0:T(8,128)}) fusion(bf16[16,128,128]{1,2,0:T(8,128)(2,1)S(1)} %copy-done.1), kind=kLoop, calls=%fused_computation.76 | loop fusion | bytes 4096000 | tf_op jit(solution)/shard_map/jit(_roll_static)/slice | solution.py:75
  77.0 1.5 %fusion.41 = (f32[16,128,124]{1,2,0:T(8,128)}, f32[16,128,124]{1,2,0:T(8,128)}) fusion(bf16[16,128,128]{1,2,0:T(8,128)(2,1)S(1)} %copy-done.1), kind=kLoop, calls=%fused_computation.72 | loop fusion | bytes 4063232 | tf_op jit(solution)/shard_map/jit(_roll_static)/slice | solution.py:75
  78.4 12.3 %all-to-all-done.2 = bf16[512,4,128]{2,1,0:T(4,128)(2,1)S(1)} async-done(((bf16[512,4,128]{2,1,0:T(4,128)(2,1)}), bf16[512,4,128]{2,1,0:T(4,128)(2,1)S(1)}, u32[]{:S(2)}, u32[]{:S(2)}) %all-to-all-start.2) | async-done | bytes 524320 | tf_op jit(solution)/shard_map/all_to_all | solution.py:67
  90.7 0.1 copy.43
  90.8 0.1 convert_bitcast_fusion
  90.9 0.1 copy.44
  91.0 1.4 %copy.45 = f32[16,128,128]{1,2,0:T(8,128)} copy(f32[16,128,128]{2,0,1:T(8,128)S(1)} %bitcast.77) | data formatting | bytes 2097152 | tf_op jit(solution)/shard_map/convert_element_type | solution.py:87
  92.6 0.0 copy-start.20
  92.6 5.9 %convolution_multiply_fusion.3 = f32[16,128,128]{2,1,0:T(8,128)S(1)} fusion(bf16[16,2048,128]{1,2,0:T(8,128)(2,1)} %all-gather.2.cloned.1.call-done, bf16[128,2048]{1,0:T(8,128)(2,1)S(1)} %copy-done.19), kind=kOutput, calls=%fused_computation.9 | convolution fusion | flops 1074003968 | bytes 9961472 | tf_op jit(solution)/shard_map/ax,yxz->yaz/dot_general | solution.py:50
  98.6 0.2 copy-done.11
  98.8 0.3 copy-done.12
  99.1 0.3 copy-done.13
  99.4 0.3 copy-done.14
  99.7 0.3 copy-done.15
  100.0 0.3 copy-done.16
  100.3 0.1 copy-done.20
  100.4 13.1 %fusion.11 = bf16[16,128,128]{1,2,0:T(8,128)(2,1)S(1)} fusion(f32[16,128,128]{1,2,0:T(8,128)S(1)} %copy-done.2, f32[16,128,128]{2,1,0:T(8,128)S(1)} %convolution_multiply_fusion.3, bf16[16,2048,128]{1,2,0:T(8,128)(2,1)} %all-gather.2.cloned.1.call-done, f32[16,128,124]{1,2,0:T(8,128)} %get-tuple-element.10, f32[16,128,4]{1,2,0:T(4,128)S(1)} %get-tuple-element.12, ...), kind=kOutput, calls=%fused_computation.16 | convolution fusion | flops 1101529088 | bytes 29360712 | tf_op jit(solution)/shard_map/ax,yxz->yaz/dot_general | solution.py:53
  113.5 1.0 copy.48
  (44 shorter events, 0.1 us)
Async XLA Ops:
  6.5 60.6 %copy-start = (bf16[512,512]{1,0:T(8,128)(2,1)S(1)}, bf16[512,512]{1,0:T(8,128)(2,1)}, u32[]{:S(2)}) copy-start(bf16[512,512]{1,0:T(8,128)(2,1)} %param.16) | copy-start | bytes 1572868
  6.5 85.9 %all-gather.2.cloned.1.call-start = ((), (), s32[]{:S(2)}) async-start(), calls=%async_computation.3 | async-start | bytes 8912896 | tf_op jit(solution)/shard_map/all_gather | solution.py:47
  8.6 38.4 %copy-start.17 = (f32[512]{0:T(512)S(1)}, f32[512]{0:T(512)}, u32[]{:S(2)}) copy-start(f32[512]{0:T(512)} %param.18) | copy-start | bytes 6148
  8.7 43.9 %copy-start.21 = (s32[32]{0:T(128)S(1)}, s32[32]{0:T(128)}, u32[]{:S(2)}) copy-start(s32[32]{0:T(128)} %param.21) | copy-start | bytes 388
  10.9 30.9 %all-to-all-start.1 = ((bf16[16,128,128]{2,0,1:T(8,128)(2,1)}), bf16[16,128,128]{2,0,1:T(8,128)(2,1)S(1)}, u32[]{:S(2)}, u32[]{:S(2)}) async-start(bf16[16,128,128]{2,0,1:T(8,128)(2,1)} %copy.40), calls=%async_computation.1 | async-start | bytes 1048576 | tf_op jit(solution)/shard_map/all_to_all | solution.py:60
  34.1 21.6 %copy-start.1 = (bf16[16,128,128]{1,2,0:T(8,128)(2,1)S(1)}, bf16[16,128,128]{1,2,0:T(8,128)(2,1)}, u32[]{:S(2)}) copy-start(bf16[16,128,128]{1,2,0:T(8,128)(2,1)} %copy.37) | copy-start | bytes 1572868
  41.8 22.5 %all-to-all-start = ((bf16[16,128,128]{2,0,1:T(8,128)(2,1)}), bf16[16,128,128]{2,0,1:T(8,128)(2,1)}, u32[]{:S(2)}, u32[]{:S(2)}) async-start(bf16[16,128,128]{2,0,1:T(8,128)(2,1)} %copy.38), calls=%async_computation | async-start | bytes 1048576 | tf_op jit(solution)/shard_map/all_to_all | solution.py:59
  52.7 14.4 %copy-start.18 = (f32[512]{0:T(512)S(1)}, f32[512]{0:T(512)}, u32[]{:S(2)}) copy-start(f32[512]{0:T(512)} %param.19) | copy-start | bytes 6148
  69.2 21.5 %all-to-all-start.2 = ((bf16[512,4,128]{2,1,0:T(4,128)(2,1)}), bf16[512,4,128]{2,1,0:T(4,128)(2,1)S(1)}, u32[]{:S(2)}, u32[]{:S(2)}) async-start(bf16[512,4,128]{2,1,0:T(4,128)(2,1)} %copy.42), calls=%async_computation.2 | async-start | bytes 1048576 | tf_op jit(solution)/shard_map/all_to_all | solution.py:67
  75.5 17.0 %copy-start.19 = (bf16[128,2048]{1,0:T(8,128)(2,1)S(1)}, bf16[128,2048]{1,0:T(8,128)(2,1)}, u32[]{:S(2)}) copy-start(bf16[128,2048]{1,0:T(8,128)(2,1)} %param.15) | copy-start | bytes 1572868
  92.4 6.1 %copy-start.2 = (f32[16,128,128]{1,2,0:T(8,128)S(1)}, f32[16,128,128]{1,2,0:T(8,128)}, u32[]{:S(2)}) copy-start(f32[16,128,128]{1,2,0:T(8,128)} %copy.45) | copy-start | bytes 3145732
  92.4 6.1 %copy-start.3 = (f32[16,128,126]{1,2,0:T(8,128)S(1)}, f32[16,128,126]{1,2,0:T(8,128)}, u32[]{:S(2)}) copy-start(f32[16,128,126]{1,2,0:T(8,128)} %get-tuple-element.21) | copy-start | bytes 3096580
  92.4 6.1 %copy-start.4 = (f32[16,128,126]{1,2,0:T(8,128)S(1)}, f32[16,128,126]{1,2,0:T(8,128)}, u32[]{:S(2)}) copy-start(f32[16,128,126]{1,2,0:T(8,128)} %get-tuple-element.22) | copy-start | bytes 3096580
  92.5 6.1 %copy-start.5 = (f32[16,128,127]{1,2,0:T(8,128)S(1)}, f32[16,128,127]{1,2,0:T(8,128)}, u32[]{:S(2)}) copy-start(f32[16,128,127]{1,2,0:T(8,128)} %get-tuple-element.29) | copy-start | bytes 3121156
  92.5 6.1 %copy-start.6 = (f32[16,128,127]{1,2,0:T(8,128)S(1)}, f32[16,128,127]{1,2,0:T(8,128)}, u32[]{:S(2)}) copy-start(f32[16,128,127]{1,2,0:T(8,128)} %get-tuple-element.30) | copy-start | bytes 3121156
  92.5 6.1 %copy-start.7 = (f32[16,128,125]{1,2,0:T(8,128)S(1)}, f32[16,128,125]{1,2,0:T(8,128)}, u32[]{:S(2)}) copy-start(f32[16,128,125]{1,2,0:T(8,128)} %get-tuple-element.13) | copy-start | bytes 3072004
  92.5 6.1 %copy-start.8 = (f32[16,128,125]{1,2,0:T(8,128)S(1)}, f32[16,128,125]{1,2,0:T(8,128)}, u32[]{:S(2)}) copy-start(f32[16,128,125]{1,2,0:T(8,128)} %get-tuple-element.14) | copy-start | bytes 3072004
  92.5 6.1 %copy-start.9 = (f32[16,128,124]{1,2,0:T(8,128)S(1)}, f32[16,128,124]{1,2,0:T(8,128)}, u32[]{:S(2)}) copy-start(f32[16,128,124]{1,2,0:T(8,128)} %get-tuple-element.5) | copy-start | bytes 3047428
  92.5 6.1 %copy-start.10 = (f32[16,128,124]{1,2,0:T(8,128)S(1)}, f32[16,128,124]{1,2,0:T(8,128)}, u32[]{:S(2)}) copy-start(f32[16,128,124]{1,2,0:T(8,128)} %get-tuple-element.6) | copy-start | bytes 3047428
  92.5 6.3 %copy-start.11 = (f32[16,128,126]{1,2,0:T(8,128)S(1)}, f32[16,128,126]{1,2,0:T(8,128)}, u32[]{:S(2)}) copy-start(f32[16,128,126]{1,2,0:T(8,128)} %get-tuple-element.25) | copy-start | bytes 3096580
  92.5 6.6 %copy-start.12 = (f32[16,128,126]{1,2,0:T(8,128)S(1)}, f32[16,128,126]{1,2,0:T(8,128)}, u32[]{:S(2)}) copy-start(f32[16,128,126]{1,2,0:T(8,128)} %get-tuple-element.26) | copy-start | bytes 3096580
  92.5 6.9 %copy-start.13 = (f32[16,128,127]{1,2,0:T(8,128)S(1)}, f32[16,128,127]{1,2,0:T(8,128)}, u32[]{:S(2)}) copy-start(f32[16,128,127]{1,2,0:T(8,128)} %get-tuple-element.33) | copy-start | bytes 3121156
  92.5 7.2 %copy-start.14 = (f32[16,128,127]{1,2,0:T(8,128)S(1)}, f32[16,128,127]{1,2,0:T(8,128)}, u32[]{:S(2)}) copy-start(f32[16,128,127]{1,2,0:T(8,128)} %get-tuple-element.34) | copy-start | bytes 3121156
  92.6 7.5 %copy-start.15 = (f32[16,128,125]{1,2,0:T(8,128)S(1)}, f32[16,128,125]{1,2,0:T(8,128)}, u32[]{:S(2)}) copy-start(f32[16,128,125]{1,2,0:T(8,128)} %get-tuple-element.17) | copy-start | bytes 3072004
  92.6 7.8 %copy-start.16 = (f32[16,128,125]{1,2,0:T(8,128)S(1)}, f32[16,128,125]{1,2,0:T(8,128)}, u32[]{:S(2)}) copy-start(f32[16,128,125]{1,2,0:T(8,128)} %get-tuple-element.18) | copy-start | bytes 3072004
  92.6 7.9 %copy-start.20 = (bf16[128,2048]{1,0:T(8,128)(2,1)S(1)}, bf16[128,2048]{1,0:T(8,128)(2,1)}, u32[]{:S(2)}) copy-start(bf16[128,2048]{1,0:T(8,128)(2,1)} %param.14) | copy-start | bytes 1572868
Sparse Core Ops, SparseCore 0:
  9.4 70.7 all-gather.1
where the time goes:
time: 122 us; the launch traced here: 121 us
  local copies, waits for them, and re-layouts  32.2 us (26%)
  waiting for transfers between devices  23.7 us (19%)
  starting transfers between devices  23.2 us (19%)
  matrix products  21.5 us (18%)
  between operations  19.3 us (16%)
  other arithmetic  1.46 us (1%)
    all_to_all x1, starting transfers between devices, on_device(): lax.all_to_all(normal_speed, 'col', split_axis=1, concat_axis=0, tiled=True)  13.2 us
    dot_general x1, matrix products, on_device(): jnp.einsum('ax,yxz->yaz', stream_first, flux_gathered, preferred_element_...  13.1 us
    all_to_all x1, waiting for transfers between devices, on_device(): lax.all_to_all(outcome, 'col', split_axis=0, concat_axis=1, tiled=True)  12.3 us
    unnamed x48, local copies, waits for them, and re-layouts  9.7 us
    slice x8, local copies, waits for them, and re-layouts, on_device(): jnp.roll(stream_full, -offset_z, 2)  9.11 us
    all_to_all x1, waiting for transfers between devices, on_device(): lax.all_to_all(stream_speed, 'col', split_axis=1, concat_axis=0, tiled=True)  6.85 us
    slice x8, local copies, waits for them, and re-layouts, on_device(): jnp.roll(flux_span, -offset_z, 2)  6.14 us
    dot_general x1, matrix products, on_device(): jnp.einsum('ax,yxz->yaz', stream_second, gathered, preferred_element_type...  5.93 us
  transfers between devices with their start and end apart: 4, of which 3 were waited for; matrix products, arithmetic and copies ran while one was open for 26% of the time, Pallas kernels for 0%

commit v1 on v0

v1 whole, which is shorter than its diff:
```python
import functools

import jax
import jax.numpy as jnp
from jax import lax
from jax.experimental import pallas as pl
from jax.experimental.pallas import tpu as pltpu
from jax.sharding import PartitionSpec as P

ZB = 4
VISCOSITY = 0.25
MESH = pl.DeviceIdType.MESH
F32 = jnp.float32
BF16 = jnp.bfloat16


def matmul(left, right):
    return jnp.dot(left, right, preferred_element_type=F32)


def swap_matrix(size):
    total = size * size
    row = lax.broadcasted_iota(jnp.int32, (total, total), 0)
    column = lax.broadcasted_iota(jnp.int32, (total, total), 1)
    same = (row // size == column % size) & (row % size == column // size)
    return jnp.where(same, 1.0, 0.0).astype(BF16)


def kernel(
    row_count,
    col_count,
    stream_hbm,
    normal_hbm,
    span_hbm,
    first_hbm,
    second_hbm,
    wall_first_hbm,
    wall_second_hbm,
    metric1_ref,
    metric2_ref,
    coef_ref,
    counts_ref,
    out_ref,
    gathered,
    normal,
    span,
    first,
    second,
    wall_first,
    wall_second,
    line_matrix,
    wall_matrix,
    lines_out,
    lines_in,
    terms_out,
    terms_in,
    total,
    swap,
    load_sem,
    ring_send,
    ring_recv,
    pair_send,
    pair_recv,
    lines_send,
    lines_recv,
    terms_send,
    terms_recv,
):
    chips = row_count // 2
    reach = chips // 2
    walls, length, planes = normal.shape
    half = walls // 2
    per_peer = length // col_count
    row = lax.axis_index("row")
    col = lax.axis_index("col")
    chip, core = row // 2, lax.rem(row, 2)
    right = lax.rem(row + 2, row_count)
    left = lax.rem(row + row_count - 2, row_count)
    sibling = row + 1 - 2 * core

    barrier = pltpu.get_barrier_semaphore()

    def greet(step, carry):
        peer = lax.rem(col + step, col_count)
        pl.semaphore_signal(barrier, inc=1, device_id=(row, peer), device_id_type=MESH)
        return carry

    for neighbour in (right, left, sibling):
        pl.semaphore_signal(barrier, inc=1, device_id=(neighbour, col), device_id_type=MESH)
    lax.fori_loop(1, col_count, greet, 0)

    pairs = (
        (stream_hbm, gathered.at[0, 0]),
        (normal_hbm, normal),
        (span_hbm, span),
        (second_hbm, second),
        (first_hbm, first),
        (wall_second_hbm, wall_second),
        (wall_first_hbm, wall_first),
    )
    loads = [pltpu.make_async_copy(a, b, load_sem.at[i]) for i, (a, b) in enumerate(pairs)]
    for load in loads:
        load.start()
    swap[...] = swap_matrix(walls)
    pl.semaphore_wait(barrier, col_count + 2)

    def up_slot(hop):
        return hop

    def down_slot(hop):
        return hop if hop == 0 or hop == reach else reach + hop

    def ring(way, part, hop):
        slot = up_slot if way == 0 else down_slot
        rows = pl.ds(part * half, half)
        source = stream_hbm.at[rows] if hop == 1 else gathered.at[0, slot(hop - 1), rows]
        return pltpu.make_async_remote_copy(
            src_ref=source,
            dst_ref=gathered.at[0, slot(hop), rows],
            send_sem=ring_send.at[way, part, hop - 1],
            recv_sem=ring_recv.at[way, part, hop - 1],
            device_id=(right if way == 0 else left, col),
            device_id_type=MESH,
        )

    def share(slot, part):
        rows = pl.ds(part * half, half)
        source = stream_hbm.at[rows] if slot == 0 else gathered.at[0, slot, rows]
        return pltpu.make_async_remote_copy(
            src_ref=source,
            dst_ref=gathered.at[1, slot, rows],
            send_sem=pair_send.at[slot, part],
            recv_sem=pair_recv.at[slot, part],
            device_id=(sibling, col),
            device_id_type=MESH,
        )

    def goes(way, part, hop):
        return hop <= (reach if way == part else reach - 1)

    order = ((0, 0), (1, 1), (0, 1), (1, 0))
    for way, part in order:
        if goes(way, part, 1):
            ring(way, part, 1).start()

    loads[0].wait()
    loads[1].wait()
    own = gathered.at[0, 0]
    for group in range(length // walls):
        rows = pl.ds(group * walls, walls)
        speed = own[:, rows, :]
        flux = speed * normal[:, rows, :]
        both = jnp.concatenate(
            [speed.reshape(walls * walls, planes), flux.reshape(walls * walls, planes)], axis=1
        )
        moved = matmul(swap[...], both).astype(BF16)
        for kind in range(2):
            piece = moved[:, kind * planes : (kind + 1) * planes]
            if per_peer <= walls:
                peers = walls // per_peer
                lines_out[pl.ds(group * peers, peers), kind] = piece.reshape(
                    peers, per_peer, walls, planes
                )
            else:
                peer, start = divmod(group * walls, per_peer)
                lines_out[peer, kind, pl.ds(start, walls)] = piece.reshape(walls, walls, planes)

    def send_lines(step, carry):
        peer = lax.rem(col + step, col_count)
        pltpu.make_async_remote_copy(
            src_ref=lines_out.at[peer],
            dst_ref=lines_in.at[col],
            send_sem=lines_send,
            recv_sem=lines_recv,
            device_id=(row, peer),
            device_id_type=MESH,
        ).start()
        return carry

    lax.fori_loop(1, col_count, send_lines, 0)
    pltpu.make_async_copy(lines_out.at[col], lines_in.at[col], lines_recv).start()
    for part in range(2):
        share(0, part).start()

    loads[2].wait()
    plane_in = lax.broadcasted_iota(jnp.int32, (planes, planes), 0)
    plane_out = lax.broadcasted_iota(jnp.int32, (planes, planes), 1)
    distance = lax.rem(plane_in - plane_out + planes, planes)
    radius = coef_ref.shape[1] // 2
    banded = []
    for kind, weight in ((1, VISCOSITY), (0, -1.0)):
        band = jnp.zeros((planes, planes), F32)
        for offset in range(-radius, radius + 1):
            value = weight * coef_ref[kind, offset + radius]
            band = jnp.where(distance == offset % planes, value, band)
        banded.append(band)
    band = jnp.concatenate(banded, axis=0)
    coarse = band.astype(BF16)
    fine = (band - coarse.astype(F32)).astype(BF16)
    band = jnp.concatenate([coarse, fine], axis=1)

    for wall in range(walls):
        speed = own[wall]
        both = jnp.concatenate([speed, speed * span[wall]], axis=1)
        result = matmul(both, band)
        total[wall] = result[:, :planes] + result[:, planes:]

    loads[3].wait()
    loads[4].wait()
    for block in range(row_count):
        columns = pl.ds(block * length, length)
        line_matrix[block, :, pl.ds(0, length)] = second[:, columns] * BF16(VISCOSITY)
        line_matrix[block, :, pl.ds(length, length)] = -first[:, columns]

    def accumulate(where, slot, part):
        if slot <= reach:
            owner = lax.rem(chip - slot + chips, chips)
        else:
            owner = lax.rem(chip + slot - reach, chips)
        owner = owner * 2 + (core if where == 0 else 1 - core)
        matrix = line_matrix[owner]
        block = gathered.at[where, slot]
        for pair in range(half // 2):
            wall = part * half + 2 * pair
            speed = jnp.concatenate([block[wall], block[wall + 1]], axis=1)
            result = matmul(matrix, jnp.concatenate([speed, speed * speed], axis=0))
            total[wall] += result[:, :planes]
            total[wall + 1] += result[:, planes:]

    def shared(slot, part):
        share(slot, part).wait_recv()
        accumulate(1, slot, part)

    for part in range(2):
        accumulate(0, 0, part)

    loads[5].wait()
    loads[6].wait()
    height = wall_first.shape[0]
    chunk = min(128, height)
    diagonal = lax.broadcasted_iota(jnp.int32, (chunk, chunk), 0) == lax.broadcasted_iota(
        jnp.int32, (chunk, chunk), 1
    )
    for start in range(0, height, chunk):
        rows = pl.ds(start, chunk)
        one = jnp.sum(jnp.where(diagonal, metric1_ref[:, rows], 0.0), axis=1, keepdims=True)
        two = jnp.sum(jnp.where(diagonal, metric2_ref[:, rows], 0.0), axis=1, keepdims=True)
        first_rows = wall_first[rows, :].astype(F32)
        second_rows = wall_second[rows, :].astype(F32)
        viscous = VISCOSITY * (one * one * second_rows + two * first_rows)
        wall_matrix[rows, pl.ds(0, height)] = viscous.astype(BF16)
        wall_matrix[rows, pl.ds(height, height)] = (-(one * first_rows)).astype(BF16)

    def wall_terms():
        pltpu.make_async_copy(lines_out, lines_in, lines_recv).wait()
        for position in range(0, per_peer, 2):
            kinds = []
            for kind in range(2):
                both = [
                    lines_in[:, kind, position + i].reshape(height, planes) for i in range(2)
                ]
                kinds.append(jnp.concatenate(both, axis=1))
            operand = jnp.concatenate(kinds, axis=0)
            result = matmul(wall_matrix[...], operand).astype(BF16)
            for i in range(2):
                terms_out[:, position + i] = result[:, i * planes : (i + 1) * planes].reshape(
                    col_count, walls, planes
                )

        def send_terms(step, carry):
            peer = lax.rem(col + step, col_count)
            pltpu.make_async_remote_copy(
                src_ref=terms_out.at[peer],
                dst_ref=terms_in.at[pl.ds(col * per_peer, per_peer)],
                send_sem=terms_send,
                recv_sem=terms_recv,
                device_id=(row, peer),
                device_id_type=MESH,
            ).start()
            return carry

        lax.fori_loop(1, col_count, send_terms, 0)
        pltpu.make_async_copy(
            terms_out.at[col], terms_in.at[pl.ds(col * per_peer, per_peer)], terms_recv
        ).start()

    pending = [(0, 0), (0, 1)]
    for hop in range(1, reach + 1):
        for stage in (order[:2], order[2:]):
            arrived = []
            for way, part in stage:
                if not goes(way, part, hop):
                    continue
                ring(way, part, hop).wait_recv()
                if goes(way, part, hop + 1):
                    ring(way, part, hop + 1).start()
                slot = (up_slot if way == 0 else down_slot)(hop)
                share(slot, part).start()
                arrived.append((slot, part))
            for slot, part in arrived:
                accumulate(0, slot, part)
            for slot, part in pending:
                shared(slot, part)
            pending = arrived
        if hop == max(reach // 2, 1):
            wall_terms()
    for slot, part in pending:
        shared(slot, part)

    position = lax.broadcasted_iota(jnp.int32, (1, planes), 1)
    limit = jnp.zeros((1, planes), jnp.int32)
    for block in range(counts_ref.shape[0]):
        limit = jnp.where(position // ZB == block, counts_ref[block], limit)
    mask = jnp.where(position % ZB < limit, 1.0, 0.0).astype(F32)

    pltpu.make_async_copy(
        terms_in, terms_in, terms_recv
    ).wait()
    for group in range(0, length // walls, 2):
        both = [
            terms_in[pl.ds((group + i) * walls, walls)].reshape(walls * walls, planes)
            for i in range(2)
        ]
        moved = matmul(swap[...], jnp.concatenate(both, axis=1))
        for i in range(2):
            rows = pl.ds((group + i) * walls, walls)
            term = moved[:, i * planes : (i + 1) * planes].reshape(walls, walls, planes)
            out_ref[:, rows, :] = (mask * (total[:, rows, :] + term)).astype(BF16)

    for hop in range(1, reach + 1):
        for way, part in order:
            if goes(way, part, hop):
                ring(way, part, hop).wait_send()
    for slot in range(chips):
        for part in range(2):
            share(slot, part).wait_send()
    others = pl.ds(0, col_count - 1)
    pltpu.make_async_copy(lines_out.at[others], lines_in.at[others], lines_send).wait()
    pltpu.make_async_copy(terms_out.at[others], terms_out.at[others], terms_send).wait()


def on_device(
    row_count,
    col_count,
    stream_speed,
    normal_speed,
    span_speed,
    stream_first,
    stream_second,
    wall_first,
    wall_second,
    metric1,
    metric2,
    span_coef,
    counts,
):
    shape = stream_speed.shape
    walls, length, planes = shape
    height = wall_first.shape[0]
    chips = row_count // 2
    reach = chips // 2
    per_peer = length // col_count
    anywhere = pl.BlockSpec(memory_space=pl.ANY)
    vector = pl.BlockSpec(memory_space=pltpu.VMEM)
    scalar = pl.BlockSpec(memory_space=pltpu.SMEM)
    exchange = (col_count, 2, per_peer, walls, planes)
    dma = pltpu.SemaphoreType.DMA
    return pl.pallas_call(
        functools.partial(kernel, row_count, col_count),
        out_shape=jax.ShapeDtypeStruct(shape, BF16),
        in_specs=[anywhere] * 7 + [vector] * 2 + [scalar] * 2,
        out_specs=vector,
        scratch_shapes=[
            pltpu.VMEM((2, chips, *shape), BF16),
            pltpu.VMEM(shape, BF16),
            pltpu.VMEM(shape, BF16),
            pltpu.VMEM(stream_first.shape, BF16),
            pltpu.VMEM(stream_second.shape, BF16),
            pltpu.VMEM(wall_first.shape, BF16),
            pltpu.VMEM(wall_second.shape, BF16),
            pltpu.VMEM((row_count, length, 2 * length), BF16),
            pltpu.VMEM((height, 2 * height), BF16),
            pltpu.VMEM(exchange, BF16),
            pltpu.VMEM(exchange, BF16),
            pltpu.VMEM((col_count, per_peer, walls, planes), BF16),
            pltpu.VMEM((length, walls, planes), BF16),
            pltpu.VMEM(shape, F32),
            pltpu.VMEM((walls * walls, walls * walls), BF16),
            dma((7,)),
            dma((2, 2, reach)),
            dma((2, 2, reach)),
            dma((chips, 2)),
            dma((chips, 2)),
            dma,
            dma,
            dma,
            dma,
        ],
        compiler_params=pltpu.CompilerParams(
            collective_id=0, has_side_effects=True, vmem_limit_bytes=48 * 2**20
        ),
    )(
        stream_speed,
        normal_speed,
        span_speed,
        stream_first,
        stream_second,
        wall_first,
        wall_second,
        metric1.reshape(1, -1),
        metric2.reshape(1, -1),
        span_coef,
        counts,
    )


def solution(mesh):
    placed = (
        P("col", "row", None),
        P("col", "row", None),
        P("col", "row", None),
        P("row", None),
        P("row", None),
        P(),
        P(),
        P(),
        P(),
        P(),
        P(),
    )
    return jax.shard_map(
        functools.partial(on_device, mesh.shape["row"], mesh.shape["col"]),
        mesh=mesh,
        in_specs=placed,
        out_specs=P("col", "row", None),
        check_vma=False,
    )
```

time: 122 us -> 70.3 us (0.58)
  the two profiles are of different devices: /device:TPU:8 before, /device:TPU:1 now
where the time goes in v1:
time: 70.3 us; the launch traced here: 69.8 us
  Pallas kernels  60.3 us (86%)
  local copies, waits for them, and re-layouts  9.46 us (13%)
    pallas_call x1, Pallas kernels, on_device(): pl.pallas_call(functools.partial(kernel, row_count, col_count), out_shape...  60.3 us
    unnamed x23, local copies, waits for them, and re-layouts  9.46 us

profile of v1, /device:TPU:1, one launch (start us, length us, event | category | flops | bytes accessed | tf_op | source)
XLA Modules:
  0.0 69.8 jit_solution(2701500894010049415)
XLA Ops:
  0.0 0.0 copy-start.7
  0.0 0.0 copy-start.9
  0.0 0.0 copy-start.10
  0.0 0.7 copy-done.7
  0.7 0.0 copy-done.9
  0.7 0.0 copy-done.10
  0.7 0.0 copy-start
  0.7 1.0 %copy-done = bf16[16,128,128]{2,1,0:T(8,128)(2,1)S(1)} copy-done((bf16[16,128,128]{2,1,0:T(8,128)(2,1)S(1)}, bf16[16,128,128]{2,1,0:T(8,128)(2,1)}, u32[]{:S(2)}) %copy-start) | copy-done | bytes 524312
  1.7 0.0 copy-start.1
  1.7 1.0 %copy-done.1 = bf16[16,128,128]{2,1,0:T(8,128)(2,1)S(1)} copy-done((bf16[16,128,128]{2,1,0:T(8,128)(2,1)S(1)}, bf16[16,128,128]{2,1,0:T(8,128)(2,1)}, u32[]{:S(2)}) %copy-start.1) | copy-done | bytes 524312
  2.8 0.0 copy-start.2
  2.8 1.0 %copy-done.2 = bf16[16,128,128]{2,1,0:T(8,128)(2,1)S(1)} copy-done((bf16[16,128,128]{2,1,0:T(8,128)(2,1)S(1)}, bf16[16,128,128]{2,1,0:T(8,128)(2,1)}, u32[]{:S(2)}) %copy-start.2) | copy-done | bytes 524312
  3.8 0.0 copy-start.3
  3.8 1.0 %copy-done.3 = bf16[128,2048]{1,0:T(8,128)(2,1)S(1)} copy-done((bf16[128,2048]{1,0:T(8,128)(2,1)S(1)}, bf16[128,2048]{1,0:T(8,128)(2,1)}, u32[]{:S(2)}) %copy-start.3) | copy-done | bytes 524312
  4.9 0.0 copy-start.4
  4.9 1.0 %copy-done.4 = bf16[128,2048]{1,0:T(8,128)(2,1)S(1)} copy-done((bf16[128,2048]{1,0:T(8,128)(2,1)S(1)}, bf16[128,2048]{1,0:T(8,128)(2,1)}, u32[]{:S(2)}) %copy-start.4) | copy-done | bytes 524312
  5.9 0.0 copy-start.5
  5.9 1.0 %copy-done.5 = bf16[512,512]{1,0:T(8,128)(2,1)S(1)} copy-done((bf16[512,512]{1,0:T(8,128)(2,1)S(1)}, bf16[512,512]{1,0:T(8,128)(2,1)}, u32[]{:S(2)}) %copy-start.5) | copy-done | bytes 524312
  7.0 0.0 copy-start.6
  7.0 1.0 %copy-done.6 = bf16[512,512]{1,0:T(8,128)(2,1)S(1)} copy-done((bf16[512,512]{1,0:T(8,128)(2,1)S(1)}, bf16[512,512]{1,0:T(8,128)(2,1)}, u32[]{:S(2)}) %copy-start.6) | copy-done | bytes 524312
  8.0 0.0 copy-start.8
  8.0 0.7 copy-done.8
  8.7 60.3 %shard_map.109 = bf16[16,128,128]{2,1,0:T(8,128)(2,1)S(1)} custom-call(bf16[16,128,128]{2,1,0:T(8,128)(2,1)S(1)} %copy-done, bf16[16,128,128]{2,1,0:T(8,128)(2,1)S(1)} %copy-done.1, bf16[16,128,128]{2,1,0:T(8,128)(2,1)S(1)} %copy-done.2, bf16[128,2048]{1,0:T(8,128)(2,1)S(1)} %copy-done.3, bf16[128,2048]{1,0:T(8,128)(2,1)S(1)} %copy-done.4, ...), custom_call_target="tpu_custom_call" | custom-call | tf_op jit(solution)/shard_map/pallas_call | solution.py:368
  69.0 0.8 %copy.13 = bf16[16,128,128]{2,1,0:T(8,128)(2,1)} copy(bf16[16,128,128]{2,1,0:T(8,128)(2,1)S(1)} %shard_map.109) | data formatting | bytes 1048576
Async XLA Ops:
  0.0 0.7 copy-start.7
  0.0 0.7 copy-start.9
  0.0 0.7 copy-start.10
  0.7 1.0 %copy-start = (bf16[16,128,128]{2,1,0:T(8,128)(2,1)S(1)}, bf16[16,128,128]{2,1,0:T(8,128)(2,1)}, u32[]{:S(2)}) copy-start(bf16[16,128,128]{2,1,0:T(8,128)(2,1)} %stream_hbm.1) | copy-start | bytes 1572868
  1.7 1.0 %copy-start.1 = (bf16[16,128,128]{2,1,0:T(8,128)(2,1)S(1)}, bf16[16,128,128]{2,1,0:T(8,128)(2,1)}, u32[]{:S(2)}) copy-start(bf16[16,128,128]{2,1,0:T(8,128)(2,1)} %normal_hbm.1) | copy-start | bytes 1572868
  2.8 1.0 %copy-start.2 = (bf16[16,128,128]{2,1,0:T(8,128)(2,1)S(1)}, bf16[16,128,128]{2,1,0:T(8,128)(2,1)}, u32[]{:S(2)}) copy-start(bf16[16,128,128]{2,1,0:T(8,128)(2,1)} %span_hbm.1) | copy-start | bytes 1572868
  3.8 1.0 %copy-start.3 = (bf16[128,2048]{1,0:T(8,128)(2,1)S(1)}, bf16[128,2048]{1,0:T(8,128)(2,1)}, u32[]{:S(2)}) copy-start(bf16[128,2048]{1,0:T(8,128)(2,1)} %first_hbm.1) | copy-start | bytes 1572868
  4.9 1.0 %copy-start.4 = (bf16[128,2048]{1,0:T(8,128)(2,1)S(1)}, bf16[128,2048]{1,0:T(8,128)(2,1)}, u32[]{:S(2)}) copy-start(bf16[128,2048]{1,0:T(8,128)(2,1)} %second_hbm.1) | copy-start | bytes 1572868
  5.9 1.0 %copy-start.5 = (bf16[512,512]{1,0:T(8,128)(2,1)S(1)}, bf16[512,512]{1,0:T(8,128)(2,1)}, u32[]{:S(2)}) copy-start(bf16[512,512]{1,0:T(8,128)(2,1)} %wall_first_hbm.1) | copy-start | bytes 1572868
  7.0 1.0 %copy-start.6 = (bf16[512,512]{1,0:T(8,128)(2,1)S(1)}, bf16[512,512]{1,0:T(8,128)(2,1)}, u32[]{:S(2)}) copy-start(bf16[512,512]{1,0:T(8,128)(2,1)} %wall_second_hbm.1) | copy-start | bytes 1572868
  8.0 0.7 copy-start.8

commit v2 on v1

--- a/solution.py
+++ b/solution.py
@@ -36,11 +36,11 @@
     second_hbm,
     wall_first_hbm,
     wall_second_hbm,
-    metric1_ref,
-    metric2_ref,
-    coef_ref,
-    counts_ref,
-    out_ref,
+    metric1_hbm,
+    metric2_hbm,
+    coef_hbm,
+    counts_hbm,
+    out_hbm,
     gathered,
     normal,
     span,
@@ -56,6 +56,11 @@
     terms_in,
     total,
     swap,
+    out_ref,
+    metric1_ref,
+    metric2_ref,
+    coef_ref,
+    counts_ref,
     load_sem,
     ring_send,
     ring_recv,
@@ -65,11 +70,15 @@
     lines_recv,
     terms_send,
     terms_recv,
+    early_ready,
+    all_ready,
+    store_sem,
 ):
     chips = row_count // 2
     reach = chips // 2
     walls, length, planes = normal.shape
-    half = walls // 2
+    part_count = 4
+    depth = walls // part_count
     per_peer = length // col_count
     row = lax.axis_index("row")
     col = lax.axis_index("col")
@@ -78,16 +87,18 @@
     left = lax.rem(row + row_count - 2, row_count)
     sibling = row + 1 - 2 * core
 
+    middle = col_count // 2
+    first_leader, last_leader = middle - 1, col_count - 1
+    early, late = col < middle, col >= middle
     barrier = pltpu.get_barrier_semaphore()
 
-    def greet(step, carry):
-        peer = lax.rem(col + step, col_count)
-        pl.semaphore_signal(barrier, inc=1, device_id=(row, peer), device_id_type=MESH)
-        return carry
+    def signal(semaphore, place):
+        pl.semaphore_signal(semaphore, inc=1, device_id=place, device_id_type=MESH)
 
     for neighbour in (right, left, sibling):
-        pl.semaphore_signal(barrier, inc=1, device_id=(neighbour, col), device_id_type=MESH)
-    lax.fori_loop(1, col_count, greet, 0)
+        signal(barrier, (neighbour, col))
+    pl.when(early & (col != first_leader))(lambda: signal(barrier, (row, first_leader)))
+    pl.when(late & (col != last_leader))(lambda: signal(barrier, (row, last_leader)))
 
     pairs = (
         (stream_hbm, gathered.at[0, 0]),
@@ -97,12 +108,48 @@
         (first_hbm, first),
         (wall_second_hbm, wall_second),
         (wall_first_hbm, wall_first),
+        (coef_hbm, coef_ref),
+        (metric1_hbm, metric1_ref),
+        (metric2_hbm, metric2_ref),
+        (counts_hbm, counts_ref),
     )
     loads = [pltpu.make_async_copy(a, b, load_sem.at[i]) for i, (a, b) in enumerate(pairs)]
     for load in loads:
         load.start()
     swap[...] = swap_matrix(walls)
-    pl.semaphore_wait(barrier, col_count + 2)
+
+    @pl.when(early & (col != first_leader))
+    def _():
+        pl.semaphore_wait(barrier, 3)
+
+    @pl.when(col == first_leader)
+    def _():
+        pl.semaphore_wait(barrier, 3 + middle - 1)
+
+        def tell_late(peer, carry):
+            signal(barrier, (row, peer))
+            return carry
+
+        def tell_early(peer, carry):
+            signal(early_ready, (row, peer))
+            return carry
+
+        lax.fori_loop(middle, col_count, tell_late, 0)
+        lax.fori_loop(0, middle - 1, tell_early, 0)
+
+    @pl.when(late & (col != last_leader))
+    def _():
+        pl.semaphore_wait(barrier, 4)
+
+    @pl.when(col == last_leader)
+    def _():
+        pl.semaphore_wait(barrier, 4 + col_count - middle - 1)
+
+        def tell(peer, carry):
+            signal(all_ready, (row, peer))
+            return carry
+
+        lax.fori_loop(0, col_count - 1, tell, 0)
 
     def up_slot(hop):
         return hop
@@ -112,7 +159,7 @@
 
     def ring(way, part, hop):
         slot = up_slot if way == 0 else down_slot
-        rows = pl.ds(part * half, half)
+        rows = pl.ds(part * depth, depth)
         source = stream_hbm.at[rows] if hop == 1 else gathered.at[0, slot(hop - 1), rows]
         return pltpu.make_async_remote_copy(
             src_ref=source,
@@ -124,7 +171,7 @@
         )
 
     def share(slot, part):
-        rows = pl.ds(part * half, half)
+        rows = pl.ds(part * depth, depth)
         source = stream_hbm.at[rows] if slot == 0 else gathered.at[0, slot, rows]
         return pltpu.make_async_remote_copy(
             src_ref=source,
@@ -136,9 +183,9 @@
         )
 
     def goes(way, part, hop):
-        return hop <= (reach if way == part else reach - 1)
-
-    order = ((0, 0), (1, 1), (0, 1), (1, 0))
+        return hop <= (reach if way == part // (part_count // 2) else reach - 1)
+
+    order = ((0, 0), (1, 2), (0, 1), (1, 3), (0, 2), (1, 0), (0, 3), (1, 1))
     for way, part in order:
         if goes(way, part, 1):
             ring(way, part, 1).start()
@@ -165,8 +212,17 @@
                 peer, start = divmod(group * walls, per_peer)
                 lines_out[peer, kind, pl.ds(start, walls)] = piece.reshape(walls, walls, planes)
 
-    def send_lines(step, carry):
-        peer = lax.rem(col + step, col_count)
+    def exchange(send_piece, start, stop):
+        count = stop - start
+
+        def body(step, carry):
+            peer = start + lax.rem(col + step, count)
+            pl.when(peer != col)(lambda: send_piece(peer))
+            return carry
+
+        lax.fori_loop(0, count, body, 0)
+
+    def send_line(peer):
         pltpu.make_async_remote_copy(
             src_ref=lines_out.at[peer],
             dst_ref=lines_in.at[col],
@@ -175,14 +231,14 @@
             device_id=(row, peer),
             device_id_type=MESH,
         ).start()
-        return carry
-
-    lax.fori_loop(1, col_count, send_lines, 0)
+
     pltpu.make_async_copy(lines_out.at[col], lines_in.at[col], lines_recv).start()
-    for part in range(2):
+    pl.when(late)(lambda: exchange(send_line, 0, middle))
+    for part in range(part_count):
         share(0, part).start()
 
     loads[2].wait()
+    loads[7].wait()
     plane_in = lax.broadcasted_iota(jnp.int32, (planes, planes), 0)
     plane_out = lax.broadcasted_iota(jnp.int32, (planes, planes), 1)
     distance = lax.rem(plane_in - plane_out + planes, planes)
@@ -205,6 +261,11 @@
         result = matmul(both, band)
         total[wall] = result[:, :planes] + result[:, planes:]
 
+    @pl.when(late)
+    def _():
+        pl.when(col != last_leader)(lambda: pl.semaphore_wait(all_ready, 1))
+        exchange(send_line, middle, col_count)
+
     loads[3].wait()
     loads[4].wait()
     for block in range(row_count):
@@ -220,8 +281,8 @@
         owner = owner * 2 + (core if where == 0 else 1 - core)
         matrix = line_matrix[owner]
         block = gathered.at[where, slot]
-        for pair in range(half // 2):
-            wall = part * half + 2 * pair
+        for pair in range(depth // 2):
+            wall = part * depth + 2 * pair
             speed = jnp.concatenate([block[wall], block[wall + 1]], axis=1)
             result = matmul(matrix, jnp.concatenate([speed, speed * speed], axis=0))
             total[wall] += result[:, :planes]
@@ -231,11 +292,11 @@
         share(slot, part).wait_recv()
         accumulate(1, slot, part)
 
-    for part in range(2):
+    for part in range(part_count):
         accumulate(0, 0, part)
 
-    loads[5].wait()
-    loads[6].wait()
+    for load in loads[5:7] + loads[8:10]:
+        load.wait()
     height = wall_first.shape[0]
     chunk = min(128, height)
     diagonal = lax.broadcasted_iota(jnp.int32, (chunk, chunk), 0) == lax.broadcasted_iota(
@@ -267,8 +328,7 @@
                     col_count, walls, planes
                 )
 
-        def send_terms(step, carry):
-            peer = lax.rem(col + step, col_count)
+        def send_term(peer):
             pltpu.make_async_remote_copy(
                 src_ref=terms_out.at[peer],
                 dst_ref=terms_in.at[pl.ds(col * per_peer, per_peer)],
@@ -277,18 +337,22 @@
                 device_id=(row, peer),
                 device_id_type=MESH,
             ).start()
-            return carry
-
-        lax.fori_loop(1, col_count, send_terms, 0)
+
+        exchange(send_term, 0, col_count)
         pltpu.make_async_copy(
             terms_out.at[col], terms_in.at[pl.ds(col * per_peer, per_peer)], terms_recv
         ).start()
 
-    pending = [(0, 0), (0, 1)]
+    @pl.when(early)
+    def _():
+        pl.when(col != first_leader)(lambda: pl.semaphore_wait(early_ready, 1))
+        exchange(send_line, 0, middle)
+
+    pending = [(0, part) for part in range(part_count)]
     for hop in range(1, reach + 1):
-        for stage in (order[:2], order[2:]):
+        for half in range(2):
             arrived = []
-            for way, part in stage:
+            for way, part in order[half * part_count : (half + 1) * part_count]:
                 if not goes(way, part, hop):
                     continue
                 ring(way, part, hop).wait_recv()
@@ -302,11 +366,21 @@
             for slot, part in pending:
                 shared(slot, part)
             pending = arrived
-        if hop == max(reach // 2, 1):
-            wall_terms()
+            if (hop, half) == (1, 0):
+
+                @pl.when(early)
+                def _():
+                    pl.semaphore_wait(all_ready, 1)
+                    exchange(send_line, middle, col_count)
+
+            if (hop, half) == (max(reach // 2, 1), 1):
+                pl.when(late)(wall_terms)
+            if (hop, half) == (max(reach // 2 + 1, 1), 0):
+                pl.when(early)(wall_terms)
     for slot, part in pending:
         shared(slot, part)
 
+    loads[10].wait()
     position = lax.broadcasted_iota(jnp.int32, (1, planes), 1)
     limit = jnp.zeros((1, planes), jnp.int32)
     for block in range(counts_ref.shape[0]):
@@ -316,6 +390,7 @@
     pltpu.make_async_copy(
         terms_in, terms_in, terms_recv
     ).wait()
+    stores = []
     for group in range(0, length // walls, 2):
         both = [
             terms_in[pl.ds((group + i) * walls, walls)].reshape(walls * walls, planes)
@@ -326,17 +401,25 @@
             rows = pl.ds((group + i) * walls, walls)
             term = moved[:, i * planes : (i + 1) * planes].reshape(walls, walls, planes)
             out_ref[:, rows, :] = (mask * (total[:, rows, :] + term)).astype(BF16)
+        rows = pl.ds(group * walls, 2 * walls)
+        store = pltpu.make_async_copy(
+            out_ref.at[:, rows], out_hbm.at[:, rows], store_sem.at[group // 2]
+        )
+        store.start()
+        stores.append(store)
 
     for hop in range(1, reach + 1):
         for way, part in order:
             if goes(way, part, hop):
                 ring(way, part, hop).wait_send()
     for slot in range(chips):
-        for part in range(2):
+        for part in range(part_count):
             share(slot, part).wait_send()
     others = pl.ds(0, col_count - 1)
     pltpu.make_async_copy(lines_out.at[others], lines_in.at[others], lines_send).wait()
     pltpu.make_async_copy(terms_out.at[others], terms_out.at[others], terms_send).wait()
+    for store in stores:
+        store.wait()
 
 
 def on_device(
@@ -360,16 +443,14 @@
     chips = row_count // 2
     reach = chips // 2
     per_peer = length // col_count
-    anywhere = pl.BlockSpec(memory_space=pl.ANY)
-    vector = pl.BlockSpec(memory_space=pltpu.VMEM)
-    scalar = pl.BlockSpec(memory_space=pltpu.SMEM)
+    hbm = pl.BlockSpec(memory_space=pltpu.HBM)
     exchange = (col_count, 2, per_peer, walls, planes)
     dma = pltpu.SemaphoreType.DMA
     return pl.pallas_call(
         functools.partial(kernel, row_count, col_count),
         out_shape=jax.ShapeDtypeStruct(shape, BF16),
-        in_specs=[anywhere] * 7 + [vector] * 2 + [scalar] * 2,
-        out_specs=vector,
+        in_specs=[hbm] * 11,
+        out_specs=hbm,
         scratch_shapes=[
             pltpu.VMEM((2, chips, *shape), BF16),
             pltpu.VMEM(shape, BF16),
@@ -386,18 +467,26 @@
             pltpu.VMEM((length, walls, planes), BF16),
             pltpu.VMEM(shape, F32),
             pltpu.VMEM((walls * walls, walls * walls), BF16),
-            dma((7,)),
-            dma((2, 2, reach)),
-            dma((2, 2, reach)),
-            dma((chips, 2)),
-            dma((chips, 2)),
+            pltpu.VMEM(shape, BF16),
+            pltpu.VMEM((1, height), F32),
+            pltpu.VMEM((1, height), F32),
+            pltpu.SMEM(span_coef.shape, F32),
+            pltpu.SMEM(counts.shape, jnp.int32),
+            dma((11,)),
+            dma((2, 4, reach)),
+            dma((2, 4, reach)),
+            dma((chips, 4)),
+            dma((chips, 4)),
             dma,
             dma,
             dma,
             dma,
+            pltpu.SemaphoreType.REGULAR,
+            pltpu.SemaphoreType.REGULAR,
+            dma((length // walls // 2,)),
         ],
         compiler_params=pltpu.CompilerParams(
-            collective_id=0, has_side_effects=True, vmem_limit_bytes=48 * 2**20
+            collective_id=0, has_side_effects=True, vmem_limit_bytes=60 * 2**20
         ),
     )(
         stream_speed,

time: 70.3 us -> 61.2 us (0.87)
  the two profiles are of different devices: /device:TPU:1 before, /device:TPU:64 now
where the time goes in v2:
time: 61.2 us; the launch traced here: 61 us
  Pallas kernels  59.1 us (97%)
  local copies, waits for them, and re-layouts  1.89 us (3%)
    pallas_call x1, Pallas kernels, on_device(): pl.pallas_call(functools.partial(kernel, row_count, col_count), out_shape...  59.1 us
    unnamed x1, local copies, waits for them, and re-layouts  1.89 us

profile of v2, /device:TPU:64, one launch (start us, length us, event | category | flops | bytes accessed | tf_op | source)
XLA Modules:
  0.0 61.0 jit_solution(11961882033418590045)
XLA Ops:
  0.0 59.1 %shard_map.109 = bf16[16,128,128]{2,1,0:T(8,128)(2,1)} custom-call(bf16[16,128,128]{2,1,0:T(8,128)(2,1)} %stream_hbm.1, bf16[16,128,128]{2,1,0:T(8,128)(2,1)} %normal_hbm.1, bf16[16,128,128]{2,1,0:T(8,128)(2,1)} %span_hbm.1, bf16[128,2048]{1,0:T(8,128)(2,1)} %first_hbm.1, bf16[128,2048]{1,0:T(8,128)(2,1)} %second_hbm.1, bf16[512,512]{1,0:T(8,128)(2,1)} %wall_first_hbm.1, ...), custom_call_target="tpu_custom_call" | custom-call | tf_op jit(solution)/shard_map/pallas_call | solution.py:449
  59.1 1.9 %copy.13 = bf16[16,128,128]{2,1,0:T(8,128)(2,1)} copy(bf16[16,128,128]{2,1,0:T(8,128)(2,1)} %shard_map.109) | data formatting | bytes 1048576

commit v3 on v2

--- a/solution.py
+++ b/solution.py
@@ -8,6 +8,7 @@
 from jax.sharding import PartitionSpec as P
 
 ZB = 4
+TORUS_WIDTH = 4
 VISCOSITY = 0.25
 MESH = pl.DeviceIdType.MESH
 F32 = jnp.float32
@@ -72,6 +73,7 @@
     terms_recv,
     early_ready,
     all_ready,
+    late_ready,
     store_sem,
 ):
     chips = row_count // 2
@@ -86,19 +88,6 @@
     right = lax.rem(row + 2, row_count)
     left = lax.rem(row + row_count - 2, row_count)
     sibling = row + 1 - 2 * core
-
-    middle = col_count // 2
-    first_leader, last_leader = middle - 1, col_count - 1
-    early, late = col < middle, col >= middle
-    barrier = pltpu.get_barrier_semaphore()
-
-    def signal(semaphore, place):
-        pl.semaphore_signal(semaphore, inc=1, device_id=place, device_id_type=MESH)
-
-    for neighbour in (right, left, sibling):
-        signal(barrier, (neighbour, col))
-    pl.when(early & (col != first_leader))(lambda: signal(barrier, (row, first_leader)))
-    pl.when(late & (col != last_leader))(lambda: signal(barrier, (row, last_leader)))
 
     pairs = (
         (stream_hbm, gathered.at[0, 0]),
@@ -116,6 +105,25 @@
     loads = [pltpu.make_async_copy(a, b, load_sem.at[i]) for i, (a, b) in enumerate(pairs)]
     for load in loads:
         load.start()
+
+    middle = col_count // 2
+    first_leader, last_leader = middle - 1, col_count - 1
+    early, late = col < middle, col >= middle
+    width = min(TORUS_WIDTH, middle)
+    rounds = col_count // width
+    across, along = lax.rem(col, width), col // width
+    far = [0] + [w for d in range(1, rounds // 2 + 1) for w in dict.fromkeys((d, rounds - d))]
+    offsets = [(ahead, beside) for beside in range(width) for ahead in far if ahead or beside]
+    barrier = pltpu.get_barrier_semaphore()
+
+    def signal(semaphore, place):
+        pl.semaphore_signal(semaphore, inc=1, device_id=place, device_id_type=MESH)
+
+    for neighbour in (right, left, sibling):
+        signal(barrier, (neighbour, col))
+    pl.when(early & (col != first_leader))(lambda: signal(barrier, (row, first_leader)))
+    pl.when(late & (col != last_leader))(lambda: signal(barrier, (row, last_leader)))
+
     swap[...] = swap_matrix(walls)
 
     @pl.when(early & (col != first_leader))
@@ -149,7 +157,15 @@
             signal(all_ready, (row, peer))
             return carry
 
-        lax.fori_loop(0, col_count - 1, tell, 0)
+        lax.fori_loop(middle, col_count - 1, tell, 0)
+
+    @pl.when(late)
+    def _():
+        def tell(peer, carry):
+            signal(late_ready.at[along - rounds // 2], (row, peer))
+            return carry
+
+        lax.fori_loop(0, middle, tell, 0)
 
     def up_slot(hop):
         return hop
@@ -189,11 +205,42 @@
     for way, part in order:
         if goes(way, part, 1):
             ring(way, part, 1).start()
+    for part in range(part_count):
+        share(0, part).start()
+
+    def exchange(send_piece, wanted=None):
+        for ahead, beside in offsets:
+            peer = lax.rem(along + ahead, rounds) * width + lax.rem(across + beside, width)
+            if wanted is None:
+                send_piece(peer)
+            else:
+                pl.when(wanted(peer))(functools.partial(send_piece, peer))
+
+    def is_early(peer):
+        return peer < middle
+
+    def is_late(peer):
+        return peer >= middle
+
+    def send_line(chunk, peer):
+        pltpu.make_async_remote_copy(
+            src_ref=lines_out.at[chunk, peer],
+            dst_ref=lines_in.at[chunk, col],
+            send_sem=lines_send,
+            recv_sem=lines_recv.at[chunk],
+            device_id=(row, peer),
+            device_id_type=MESH,
+        ).start()
+
+    first_lines = functools.partial(send_line, 0)
+    second_lines = functools.partial(send_line, 1)
 
     loads[0].wait()
     loads[1].wait()
     own = gathered.at[0, 0]
-    for group in range(length // walls):
+    chunk_size = per_peer // 2
+
+    def make_lines(group):
         rows = pl.ds(group * walls, walls)
         speed = own[:, rows, :]
         flux = speed * normal[:, rows, :]
@@ -205,37 +252,31 @@
             piece = moved[:, kind * planes : (kind + 1) * planes]
             if per_peer <= walls:
                 peers = walls // per_peer
-                lines_out[pl.ds(group * peers, peers), kind] = piece.reshape(
-                    peers, per_peer, walls, planes
-                )
+                piece = piece.reshape(peers, 2, chunk_size, walls, planes)
+                for chunk in range(2):
+                    lines_out[chunk, pl.ds(group * peers, peers), kind] = piece[:, chunk]
             else:
-                peer, start = divmod(group * walls, per_peer)
-                lines_out[peer, kind, pl.ds(start, walls)] = piece.reshape(walls, walls, planes)
-
-    def exchange(send_piece, start, stop):
-        count = stop - start
-
-        def body(step, carry):
-            peer = start + lax.rem(col + step, count)
-            pl.when(peer != col)(lambda: send_piece(peer))
-            return carry
-
-        lax.fori_loop(0, count, body, 0)
-
-    def send_line(peer):
-        pltpu.make_async_remote_copy(
-            src_ref=lines_out.at[peer],
-            dst_ref=lines_in.at[col],
-            send_sem=lines_send,
-            recv_sem=lines_recv,
-            device_id=(row, peer),
-            device_id_type=MESH,
+                peer, rest = divmod(group * walls, per_peer)
+                chunk, start = divmod(rest, chunk_size)
+                piece = piece.reshape(walls, walls, planes)
+                lines_out[chunk, peer, kind, pl.ds(start, walls)] = piece
+
+    groups = length // walls
+    for group in range(groups // 2):
+        make_lines(group)
+    pl.when(late)(lambda: exchange(first_lines, is_early))
+    for group in range(groups // 2, groups):
+        make_lines(group)
+    for chunk in range(2):
+        pltpu.make_async_copy(
+            lines_out.at[chunk, col], lines_in.at[chunk, col], lines_recv.at[chunk]
         ).start()
 
-    pltpu.make_async_copy(lines_out.at[col], lines_in.at[col], lines_recv).start()
-    pl.when(late)(lambda: exchange(send_line, 0, middle))
-    for part in range(part_count):
-        share(0, part).start()
+    @pl.when(late)
+    def _():
+        pl.when(col != last_leader)(lambda: pl.semaphore_wait(all_ready, 1))
+        exchange(first_lines, is_late)
+        exchange(second_lines)
 
     loads[2].wait()
     loads[7].wait()
@@ -261,11 +302,6 @@
         result = matmul(both, band)
         total[wall] = result[:, :planes] + result[:, planes:]
 
-    @pl.when(late)
-    def _():
-        pl.when(col != last_leader)(lambda: pl.semaphore_wait(all_ready, 1))
-        exchange(send_line, middle, col_count)
-
     loads[3].wait()
     loads[4].wait()
     for block in range(row_count):
@@ -312,41 +348,65 @@
         wall_matrix[rows, pl.ds(0, height)] = viscous.astype(BF16)
         wall_matrix[rows, pl.ds(height, height)] = (-(one * first_rows)).astype(BF16)
 
-    def wall_terms():
-        pltpu.make_async_copy(lines_out, lines_in, lines_recv).wait()
-        for position in range(0, per_peer, 2):
+    def wall_terms(chunk):
+        pltpu.make_async_copy(lines_out.at[chunk], lines_in.at[chunk], lines_recv.at[chunk]).wait()
+        for position in range(0, chunk_size, 2):
             kinds = []
             for kind in range(2):
                 both = [
-                    lines_in[:, kind, position + i].reshape(height, planes) for i in range(2)
+                    lines_in[chunk, :, kind, position + i].reshape(height, planes)
+                    for i in range(2)
                 ]
                 kinds.append(jnp.concatenate(both, axis=1))
             operand = jnp.concatenate(kinds, axis=0)
             result = matmul(wall_matrix[...], operand).astype(BF16)
             for i in range(2):
-                terms_out[:, position + i] = result[:, i * planes : (i + 1) * planes].reshape(
-                    col_count, walls, planes
-                )
+                terms_out[chunk, :, position + i] = result[
+                    :, i * planes : (i + 1) * planes
+                ].reshape(col_count, walls, planes)
+
+        place = terms_in.at[pl.ds(col * per_peer + chunk * chunk_size, chunk_size)]
 
         def send_term(peer):
             pltpu.make_async_remote_copy(
-                src_ref=terms_out.at[peer],
-                dst_ref=terms_in.at[pl.ds(col * per_peer, per_peer)],
+                src_ref=terms_out.at[chunk, peer],
+                dst_ref=place,
                 send_sem=terms_send,
                 recv_sem=terms_recv,
                 device_id=(row, peer),
                 device_id_type=MESH,
             ).start()
 
-        exchange(send_term, 0, col_count)
-        pltpu.make_async_copy(
-            terms_out.at[col], terms_in.at[pl.ds(col * per_peer, per_peer)], terms_recv
-        ).start()
+        exchange(send_term)
+        pltpu.make_async_copy(terms_out.at[chunk, col], place, terms_recv).start()
+
+    first_quarter = col < middle // 2
+    second_quarter = early & (col >= middle // 2)
 
     @pl.when(early)
     def _():
         pl.when(col != first_leader)(lambda: pl.semaphore_wait(early_ready, 1))
-        exchange(send_line, 0, middle)
+        exchange(first_lines, is_early)
+
+    def lines_to_late():
+        for plane in range(rounds // 2):
+            pl.semaphore_wait(late_ready.at[plane], width)
+            for beside in range(width):
+                first_lines(middle + plane * width + lax.rem(across + beside, width))
+        exchange(second_lines)
+
+    pl.when(second_quarter)(lines_to_late)
+    slots = {
+        (1, 0): [(first_quarter, lines_to_late)],
+        (1, 1): [(late, functools.partial(wall_terms, 0))],
+        (2, 0): [(second_quarter, functools.partial(wall_terms, 0))],
+        (2, 1): [
+            (first_quarter, functools.partial(wall_terms, 0)),
+            (late, functools.partial(wall_terms, 1)),
+        ],
+        (3, 0): [(second_quarter, functools.partial(wall_terms, 1))],
+        (3, 1): [(first_quarter, functools.partial(wall_terms, 1))],
+    }
 
     pending = [(0, part) for part in range(part_count)]
     for hop in range(1, reach + 1):
@@ -366,17 +426,10 @@
             for slot, part in pending:
                 shared(slot, part)
             pending = arrived
-            if (hop, half) == (1, 0):
-
-                @pl.when(early)
-                def _():
-                    pl.semaphore_wait(all_ready, 1)
-                    exchange(send_line, middle, col_count)
-
-            if (hop, half) == (max(reach // 2, 1), 1):
-                pl.when(late)(wall_terms)
-            if (hop, half) == (max(reach // 2 + 1, 1), 0):
-                pl.when(early)(wall_terms)
+            for (at_hop, at_half), actions in slots.items():
+                if (min(at_hop, reach), at_half) == (hop, half):
+                    for condition, action in actions:
+                        pl.when(condition)(action)
     for slot, part in pending:
         shared(slot, part)
 
@@ -416,8 +469,8 @@
         for part in range(part_count):
             share(slot, part).wait_send()
     others = pl.ds(0, col_count - 1)
-    pltpu.make_async_copy(lines_out.at[others], lines_in.at[others], lines_send).wait()
-    pltpu.make_async_copy(terms_out.at[others], terms_out.at[others], terms_send).wait()
+    pltpu.make_async_copy(lines_out.at[:, others], lines_in.at[:, others], lines_send).wait()
+    pltpu.make_async_copy(terms_out.at[:, others], terms_out.at[:, others], terms_send).wait()
     for store in stores:
         store.wait()
 
@@ -444,7 +497,7 @@
     reach = chips // 2
     per_peer = length // col_count
     hbm = pl.BlockSpec(memory_space=pltpu.HBM)
-    exchange = (col_count, 2, per_peer, walls, planes)
+    exchange = (2, col_count, 2, per_peer // 2, walls, planes)
     dma = pltpu.SemaphoreType.DMA
     return pl.pallas_call(
         functools.partial(kernel, row_count, col_count),
@@ -463,7 +516,7 @@
             pltpu.VMEM((height, 2 * height), BF16),
             pltpu.VMEM(exchange, BF16),
             pltpu.VMEM(exchange, BF16),
-            pltpu.VMEM((col_count, per_peer, walls, planes), BF16),
+            pltpu.VMEM((2, col_count, per_peer // 2, walls, planes), BF16),
             pltpu.VMEM((length, walls, planes), BF16),
             pltpu.VMEM(shape, F32),
             pltpu.VMEM((walls * walls, walls * walls), BF16),
@@ -478,11 +531,12 @@
             dma((chips, 4)),
             dma((chips, 4)),
             dma,
-            dma,
+            dma((2,)),
             dma,
             dma,
             pltpu.SemaphoreType.REGULAR,
             pltpu.SemaphoreType.REGULAR,
+            pltpu.SemaphoreType.REGULAR((max(col_count // TORUS_WIDTH, 2) // 2,)),
             dma((length // walls // 2,)),
         ],
         compiler_params=pltpu.CompilerParams(

time: 61.2 us -> 58.3 us (0.953)
  the two profiles are of different devices: /device:TPU:64 before, /device:TPU:66 now
where the time goes in v3:
time: 58.3 us; the launch traced here: 58.1 us
  Pallas kernels  56.2 us (96%)
  local copies, waits for them, and re-layouts  1.89 us (3%)
    pallas_call x1, Pallas kernels, on_device(): pl.pallas_call(functools.partial(kernel, row_count, col_count), out_shape...  56.2 us
    unnamed x1, local copies, waits for them, and re-layouts  1.89 us

profile of v3, /device:TPU:66, one launch (start us, length us, event | category | flops | bytes accessed | tf_op | source)
XLA Modules:
  0.0 58.1 jit_solution(287062978344442553)
XLA Ops:
  0.0 56.2 %shard_map.109 = bf16[16,128,128]{2,1,0:T(8,128)(2,1)} custom-call(bf16[16,128,128]{2,1,0:T(8,128)(2,1)} %stream_hbm.1, bf16[16,128,128]{2,1,0:T(8,128)(2,1)} %normal_hbm.1, bf16[16,128,128]{2,1,0:T(8,128)(2,1)} %span_hbm.1, bf16[128,2048]{1,0:T(8,128)(2,1)} %first_hbm.1, bf16[128,2048]{1,0:T(8,128)(2,1)} %second_hbm.1, bf16[512,512]{1,0:T(8,128)(2,1)} %wall_first_hbm.1, ...), custom_call_target="tpu_custom_call" | custom-call | tf_op jit(solution)/shard_map/pallas_call | solution.py:502
  56.2 1.9 %copy.13 = bf16[16,128,128]{2,1,0:T(8,128)(2,1)} copy(bf16[16,128,128]{2,1,0:T(8,128)(2,1)} %shard_map.109) | data formatting | bytes 1048576

commit v4 on v3

--- a/solution.py
+++ b/solution.py
@@ -41,7 +41,7 @@
     metric2_hbm,
     coef_hbm,
     counts_hbm,
-    out_hbm,
+    out_ref,
     gathered,
     normal,
     span,
@@ -57,7 +57,6 @@
     terms_in,
     total,
     swap,
-    out_ref,
     metric1_ref,
     metric2_ref,
     coef_ref,
@@ -74,7 +73,6 @@
     early_ready,
     all_ready,
     late_ready,
-    store_sem,
 ):
     chips = row_count // 2
     reach = chips // 2
@@ -202,11 +200,13 @@
         return hop <= (reach if way == part // (part_count // 2) else reach - 1)
 
     order = ((0, 0), (1, 2), (0, 1), (1, 3), (0, 2), (1, 0), (0, 3), (1, 1))
-    for way, part in order:
-        if goes(way, part, 1):
-            ring(way, part, 1).start()
-    for part in range(part_count):
-        share(0, part).start()
+    def start_ring(turn):
+        for way, part in order[2 * turn : 2 * turn + 2]:
+            if goes(way, part, 1):
+                ring(way, part, 1).start()
+        share(0, turn).start()
+
+    start_ring(0)
 
     def exchange(send_piece, wanted=None):
         for ahead, beside in offsets:
@@ -250,33 +250,40 @@
         moved = matmul(swap[...], both).astype(BF16)
         for kind in range(2):
             piece = moved[:, kind * planes : (kind + 1) * planes]
-            if per_peer <= walls:
-                peers = walls // per_peer
-                piece = piece.reshape(peers, 2, chunk_size, walls, planes)
-                for chunk in range(2):
-                    lines_out[chunk, pl.ds(group * peers, peers), kind] = piece[:, chunk]
+            chunk, rest = divmod(group * walls, length // 2)
+            if chunk_size <= walls:
+                peers = walls // chunk_size
+                lines_out[chunk, pl.ds(rest // chunk_size, peers), kind] = piece.reshape(
+                    peers, chunk_size, walls, planes
+                )
             else:
-                peer, rest = divmod(group * walls, per_peer)
-                chunk, start = divmod(rest, chunk_size)
-                piece = piece.reshape(walls, walls, planes)
-                lines_out[chunk, peer, kind, pl.ds(start, walls)] = piece
+                peer, start = divmod(rest, chunk_size)
+                lines_out[chunk, peer, kind, pl.ds(start, walls)] = piece.reshape(
+                    walls, walls, planes
+                )
 
     groups = length // walls
     for group in range(groups // 2):
         make_lines(group)
-    pl.when(late)(lambda: exchange(first_lines, is_early))
-    for group in range(groups // 2, groups):
-        make_lines(group)
-    for chunk in range(2):
+
+    def keep_line(chunk):
         pltpu.make_async_copy(
             lines_out.at[chunk, col], lines_in.at[chunk, col], lines_recv.at[chunk]
         ).start()
+
+    keep_line(0)
+    start_ring(1)
+    pl.when(late)(lambda: exchange(first_lines, is_early))
+    start_ring(2)
+    for group in range(groups // 2, groups):
+        make_lines(group)
+    keep_line(1)
+    start_ring(3)
 
     @pl.when(late)
     def _():
         pl.when(col != last_leader)(lambda: pl.semaphore_wait(all_ready, 1))
         exchange(first_lines, is_late)
-        exchange(second_lines)
 
     loads[2].wait()
     loads[7].wait()
@@ -302,6 +309,22 @@
         result = matmul(both, band)
         total[wall] = result[:, :planes] + result[:, planes:]
 
+    first_quarter = col < middle // 2
+    second_quarter = early & (col >= middle // 2)
+
+    @pl.when(early)
+    def _():
+        pl.when(col != first_leader)(lambda: pl.semaphore_wait(early_ready, 1))
+        exchange(first_lines, is_early)
+
+    def lines_to_late():
+        for plane in range(rounds // 2):
+            pl.semaphore_wait(late_ready.at[plane], width)
+            for beside in range(width):
+                first_lines(middle + plane * width + lax.rem(across + beside, width))
+
+    pl.when(second_quarter)(lines_to_late)
+
     loads[3].wait()
     loads[4].wait()
     for block in range(row_count):
@@ -365,47 +388,66 @@
                     :, i * planes : (i + 1) * planes
                 ].reshape(col_count, walls, planes)
 
-        place = terms_in.at[pl.ds(col * per_peer + chunk * chunk_size, chunk_size)]
+        place = terms_in.at[chunk, pl.ds(col * chunk_size, chunk_size)]
 
         def send_term(peer):
             pltpu.make_async_remote_copy(
                 src_ref=terms_out.at[chunk, peer],
                 dst_ref=place,
                 send_sem=terms_send,
-                recv_sem=terms_recv,
+                recv_sem=terms_recv.at[chunk],
                 device_id=(row, peer),
                 device_id_type=MESH,
             ).start()
 
         exchange(send_term)
-        pltpu.make_async_copy(terms_out.at[chunk, col], place, terms_recv).start()
-
-    first_quarter = col < middle // 2
-    second_quarter = early & (col >= middle // 2)
-
-    @pl.when(early)
-    def _():
-        pl.when(col != first_leader)(lambda: pl.semaphore_wait(early_ready, 1))
-        exchange(first_lines, is_early)
-
-    def lines_to_late():
-        for plane in range(rounds // 2):
-            pl.semaphore_wait(late_ready.at[plane], width)
-            for beside in range(width):
-                first_lines(middle + plane * width + lax.rem(across + beside, width))
-        exchange(second_lines)
-
-    pl.when(second_quarter)(lines_to_late)
+        pltpu.make_async_copy(terms_out.at[chunk, col], place, terms_recv.at[chunk]).start()
+
+    def add_terms(chunk):
+        pltpu.make_async_copy(terms_in.at[chunk], terms_in.at[chunk], terms_recv.at[chunk]).wait()
+        for group in range(0, groups // 2, 2):
+            both = [
+                terms_in[chunk, pl.ds((group + i) * walls, walls)].reshape(walls * walls, planes)
+                for i in range(2)
+            ]
+            moved = matmul(swap[...], jnp.concatenate(both, axis=1))
+            for i in range(2):
+                rows = pl.ds(chunk * (length // 2) + (group + i) * walls, walls)
+                term = moved[:, i * planes : (i + 1) * planes].reshape(walls, walls, planes)
+                total[:, rows, :] += term
+
+    send_second = functools.partial(exchange, second_lines)
+    wall_first_half = functools.partial(wall_terms, 0)
+    wall_second_half = functools.partial(wall_terms, 1)
+    add_first_half = functools.partial(add_terms, 0)
+    add_second_half = functools.partial(add_terms, 1)
     slots = {
-        (1, 0): [(first_quarter, lines_to_late)],
-        (1, 1): [(late, functools.partial(wall_terms, 0))],
-        (2, 0): [(second_quarter, functools.partial(wall_terms, 0))],
+        (1, 0): [
+            (first_quarter, lines_to_late),
+            (second_quarter, send_second),
+            (late, send_second),
+        ],
+        (1, 1): [
+            (first_quarter, send_second),
+        ],
+        (2, 0): [
+            (second_quarter, wall_first_half),
+            (late, wall_first_half),
+        ],
         (2, 1): [
-            (first_quarter, functools.partial(wall_terms, 0)),
-            (late, functools.partial(wall_terms, 1)),
-        ],
-        (3, 0): [(second_quarter, functools.partial(wall_terms, 1))],
-        (3, 1): [(first_quarter, functools.partial(wall_terms, 1))],
+            (first_quarter, wall_first_half),
+            (late, wall_second_half),
+        ],
+        (3, 0): [
+            (second_quarter, wall_second_half),
+        ],
+        (3, 1): [
+            (first_quarter, wall_second_half),
+        ],
+        (4, 0): [
+            (None, add_first_half),
+            (late, add_second_half),
+        ],
     }
 
     pending = [(0, part) for part in range(part_count)]
@@ -429,7 +471,10 @@
             for (at_hop, at_half), actions in slots.items():
                 if (min(at_hop, reach), at_half) == (hop, half):
                     for condition, action in actions:
-                        pl.when(condition)(action)
+                        if condition is None:
+                            action()
+                        else:
+                            pl.when(condition)(action)
     for slot, part in pending:
         shared(slot, part)
 
@@ -440,26 +485,10 @@
         limit = jnp.where(position // ZB == block, counts_ref[block], limit)
     mask = jnp.where(position % ZB < limit, 1.0, 0.0).astype(F32)
 
-    pltpu.make_async_copy(
-        terms_in, terms_in, terms_recv
-    ).wait()
-    stores = []
-    for group in range(0, length // walls, 2):
-        both = [
-            terms_in[pl.ds((group + i) * walls, walls)].reshape(walls * walls, planes)
-            for i in range(2)
-        ]
-        moved = matmul(swap[...], jnp.concatenate(both, axis=1))
-        for i in range(2):
-            rows = pl.ds((group + i) * walls, walls)
-            term = moved[:, i * planes : (i + 1) * planes].reshape(walls, walls, planes)
-            out_ref[:, rows, :] = (mask * (total[:, rows, :] + term)).astype(BF16)
-        rows = pl.ds(group * walls, 2 * walls)
-        store = pltpu.make_async_copy(
-            out_ref.at[:, rows], out_hbm.at[:, rows], store_sem.at[group // 2]
-        )
-        store.start()
-        stores.append(store)
+    pl.when(early)(add_second_half)
+    for start in range(0, walls, depth):
+        rows = pl.ds(start, depth)
+        out_ref[rows] = (mask * total[rows]).astype(BF16)
 
     for hop in range(1, reach + 1):
         for way, part in order:
@@ -471,8 +500,6 @@
     others = pl.ds(0, col_count - 1)
     pltpu.make_async_copy(lines_out.at[:, others], lines_in.at[:, others], lines_send).wait()
     pltpu.make_async_copy(terms_out.at[:, others], terms_out.at[:, others], terms_send).wait()
-    for store in stores:
-        store.wait()
 
 
 def on_device(
@@ -503,7 +530,7 @@
         functools.partial(kernel, row_count, col_count),
         out_shape=jax.ShapeDtypeStruct(shape, BF16),
         in_specs=[hbm] * 11,
-        out_specs=hbm,
+        out_specs=pl.BlockSpec(memory_space=pltpu.VMEM),
         scratch_shapes=[
             pltpu.VMEM((2, chips, *shape), BF16),
             pltpu.VMEM(shape, BF16),
@@ -517,10 +544,9 @@
             pltpu.VMEM(exchange, BF16),
             pltpu.VMEM(exchange, BF16),
             pltpu.VMEM((2, col_count, per_peer // 2, walls, planes), BF16),
-            pltpu.VMEM((length, walls, planes), BF16),
+            pltpu.VMEM((2, length // 2, walls, planes), BF16),
             pltpu.VMEM(shape, F32),
             pltpu.VMEM((walls * walls, walls * walls), BF16),
-            pltpu.VMEM(shape, BF16),
             pltpu.VMEM((1, height), F32),
             pltpu.VMEM((1, height), F32),
             pltpu.SMEM(span_coef.shape, F32),
@@ -533,14 +559,13 @@
             dma,
             dma((2,)),
             dma,
-            dma,
+            dma((2,)),
             pltpu.SemaphoreType.REGULAR,
             pltpu.SemaphoreType.REGULAR,
             pltpu.SemaphoreType.REGULAR((max(col_count // TORUS_WIDTH, 2) // 2,)),
-            dma((length // walls // 2,)),
         ],
         compiler_params=pltpu.CompilerParams(
-            collective_id=0, has_side_effects=True, vmem_limit_bytes=60 * 2**20
+            collective_id=0, has_side_effects=True, vmem_limit_bytes=53 * 2**20
         ),
     )(
         stream_speed,

time: 58.3 us -> 57.6 us (0.988)
  the two profiles are of different devices: /device:TPU:66 before, /device:TPU:64 now
where the time goes in v4:
time: 57.6 us; the launch traced here: 57.4 us
  Pallas kernels  55.3 us (96%)
  local copies, waits for them, and re-layouts  2.17 us (4%)
    pallas_call x1, Pallas kernels, on_device(): pl.pallas_call(functools.partial(kernel, row_count, col_count), out_shape...  55.3 us
    unnamed x9, local copies, waits for them, and re-layouts  2.17 us

profile of v4, /device:TPU:64, one launch (start us, length us, event | category | flops | bytes accessed | tf_op | source)
XLA Modules:
  0.0 57.4 jit_solution(10461932681525083348)
XLA Ops:
  0.0 0.0 copy-start
  0.0 0.0 copy-start.2
  0.0 0.0 copy-start.3
  0.0 0.7 %copy-done = f32[512]{0:T(512)S(1)} copy-done((f32[512]{0:T(512)S(1)}, f32[512]{0:T(512)}, u32[]{:S(2)}) %copy-start) | copy-done | bytes 2072
  0.7 0.0 copy-done.2
  0.7 0.0 copy-done.3
  0.7 0.0 copy-start.1
  0.7 0.7 %copy-done.1 = f32[512]{0:T(512)S(1)} copy-done((f32[512]{0:T(512)S(1)}, f32[512]{0:T(512)}, u32[]{:S(2)}) %copy-start.1) | copy-done | bytes 2072
  1.4 55.3 %shard_map.109 = bf16[16,128,128]{2,1,0:T(8,128)(2,1)S(1)} custom-call(bf16[16,128,128]{2,1,0:T(8,128)(2,1)} %stream_hbm.1, bf16[16,128,128]{2,1,0:T(8,128)(2,1)} %normal_hbm.1, bf16[16,128,128]{2,1,0:T(8,128)(2,1)} %span_hbm.1, bf16[128,2048]{1,0:T(8,128)(2,1)} %first_hbm.1, bf16[128,2048]{1,0:T(8,128)(2,1)} %second_hbm.1, bf16[512,512]{1,0:T(8,128)(2,1)} %wall_first_hbm.1, ...), custom_call_target="tpu_custom_call" | custom-call | tf_op jit(solution)/shard_map/pallas_call | solution.py:529
  56.7 0.8 %copy.13 = bf16[16,128,128]{2,1,0:T(8,128)(2,1)} copy(bf16[16,128,128]{2,1,0:T(8,128)(2,1)S(1)} %shard_map.109) | data formatting | bytes 1048576
Async XLA Ops:
  0.0 0.7 %copy-start = (f32[512]{0:T(512)S(1)}, f32[512]{0:T(512)}, u32[]{:S(2)}) copy-start(f32[512]{0:T(512)} %param.18) | copy-start | bytes 6148
  0.0 0.7 %copy-start.2 = (f32[2,9]{1,0:T(2,128)S(1)}, f32[2,9]{1,0:T(2,128)}, u32[]{:S(2)}) copy-start(f32[2,9]{1,0:T(2,128)} %coef_hbm.1) | copy-start | bytes 220
  0.0 0.7 %copy-start.3 = (s32[32]{0:T(128)S(1)}, s32[32]{0:T(128)}, u32[]{:S(2)}) copy-start(s32[32]{0:T(128)} %counts_hbm.1) | copy-start | bytes 388
  0.7 0.7 %copy-start.1 = (f32[512]{0:T(512)S(1)}, f32[512]{0:T(512)}, u32[]{:S(2)}) copy-start(f32[512]{0:T(512)} %param.19) | copy-start | bytes 6148

commit v5 on v4

--- a/solution.py
+++ b/solution.py
@@ -371,6 +371,22 @@
         wall_matrix[rows, pl.ds(0, height)] = viscous.astype(BF16)
         wall_matrix[rows, pl.ds(height, height)] = (-(one * first_rows)).astype(BF16)
 
+    def place_of(chunk):
+        return terms_in.at[chunk, pl.ds(col * chunk_size, chunk_size)]
+
+    def send_term(chunk, peer):
+        pltpu.make_async_remote_copy(
+            src_ref=terms_out.at[chunk, peer],
+            dst_ref=place_of(chunk),
+            send_sem=terms_send,
+            recv_sem=terms_recv.at[chunk],
+            device_id=(row, peer),
+            device_id_type=MESH,
+        ).start()
+
+    first_terms = functools.partial(send_term, 0)
+    second_terms = functools.partial(send_term, 1)
+
     def wall_terms(chunk):
         pltpu.make_async_copy(lines_out.at[chunk], lines_in.at[chunk], lines_recv.at[chunk]).wait()
         for position in range(0, chunk_size, 2):
@@ -388,20 +404,15 @@
                     :, i * planes : (i + 1) * planes
                 ].reshape(col_count, walls, planes)
 
-        place = terms_in.at[chunk, pl.ds(col * chunk_size, chunk_size)]
-
-        def send_term(peer):
-            pltpu.make_async_remote_copy(
-                src_ref=terms_out.at[chunk, peer],
-                dst_ref=place,
-                send_sem=terms_send,
-                recv_sem=terms_recv.at[chunk],
-                device_id=(row, peer),
-                device_id_type=MESH,
-            ).start()
-
-        exchange(send_term)
-        pltpu.make_async_copy(terms_out.at[chunk, col], place, terms_recv.at[chunk]).start()
+        if chunk == 0:
+            pl.when(late)(lambda: exchange(first_terms))
+            pl.when(early)(lambda: exchange(first_terms, is_early))
+        else:
+            exchange(second_terms)
+            pl.when(early)(lambda: exchange(first_terms, is_late))
+        pltpu.make_async_copy(
+            terms_out.at[chunk, col], place_of(chunk), terms_recv.at[chunk]
+        ).start()
 
     def add_terms(chunk):
         pltpu.make_async_copy(terms_in.at[chunk], terms_in.at[chunk], terms_recv.at[chunk]).wait()

time: 57.6 us -> 56.8 us (0.986)
  the two profiles are of different devices: /device:TPU:64 before, /device:TPU:8 now
where the time goes in v5:
time: 56.8 us; the launch traced here: 56.7 us
  Pallas kernels  54.5 us (96%)
  local copies, waits for them, and re-layouts  2.17 us (4%)
    pallas_call x1, Pallas kernels, on_device(): pl.pallas_call(functools.partial(kernel, row_count, col_count), out_shape...  54.5 us
    unnamed x9, local copies, waits for them, and re-layouts  2.17 us

profile of v5, /device:TPU:8, one launch (start us, length us, event | category | flops | bytes accessed | tf_op | source)
XLA Modules:
  0.0 56.7 jit_solution(18059172214232134624)
XLA Ops:
  0.0 0.0 copy-start
  0.0 0.0 copy-start.2
  0.0 0.0 copy-start.3
  0.0 0.7 %copy-done = f32[512]{0:T(512)S(1)} copy-done((f32[512]{0:T(512)S(1)}, f32[512]{0:T(512)}, u32[]{:S(2)}) %copy-start) | copy-done | bytes 2072
  0.7 0.0 copy-done.2
  0.7 0.0 copy-done.3
  0.7 0.0 copy-start.1
  0.7 0.7 %copy-done.1 = f32[512]{0:T(512)S(1)} copy-done((f32[512]{0:T(512)S(1)}, f32[512]{0:T(512)}, u32[]{:S(2)}) %copy-start.1) | copy-done | bytes 2072
  1.4 54.5 %shard_map.109 = bf16[16,128,128]{2,1,0:T(8,128)(2,1)S(1)} custom-call(bf16[16,128,128]{2,1,0:T(8,128)(2,1)} %stream_hbm.1, bf16[16,128,128]{2,1,0:T(8,128)(2,1)} %normal_hbm.1, bf16[16,128,128]{2,1,0:T(8,128)(2,1)} %span_hbm.1, bf16[128,2048]{1,0:T(8,128)(2,1)} %first_hbm.1, bf16[128,2048]{1,0:T(8,128)(2,1)} %second_hbm.1, bf16[512,512]{1,0:T(8,128)(2,1)} %wall_first_hbm.1, ...), custom_call_target="tpu_custom_call" | custom-call | tf_op jit(solution)/shard_map/pallas_call | solution.py:540
  55.9 0.8 %copy.13 = bf16[16,128,128]{2,1,0:T(8,128)(2,1)} copy(bf16[16,128,128]{2,1,0:T(8,128)(2,1)S(1)} %shard_map.109) | data formatting | bytes 1048576
Async XLA Ops:
  0.0 0.7 %copy-start = (f32[512]{0:T(512)S(1)}, f32[512]{0:T(512)}, u32[]{:S(2)}) copy-start(f32[512]{0:T(512)} %param.18) | copy-start | bytes 6148
  0.0 0.7 %copy-start.2 = (f32[2,9]{1,0:T(2,128)S(1)}, f32[2,9]{1,0:T(2,128)}, u32[]{:S(2)}) copy-start(f32[2,9]{1,0:T(2,128)} %coef_hbm.1) | copy-start | bytes 220
  0.0 0.7 %copy-start.3 = (s32[32]{0:T(128)S(1)}, s32[32]{0:T(128)}, u32[]{:S(2)}) copy-start(s32[32]{0:T(128)} %counts_hbm.1) | copy-start | bytes 388
  0.7 0.7 %copy-start.1 = (f32[512]{0:T(512)S(1)}, f32[512]{0:T(512)}, u32[]{:S(2)}) copy-start(f32[512]{0:T(512)} %param.19) | copy-start | bytes 6148
